TPU v7x, 32 devices: a whole 2x2x4 slice. The times are simulated.
32 devices in a mesh: qr: 4 (over z), qc: 4 (over x, core), grp: 2 (over y).
Axes of the slice: x: 2, y: 2, z: 4, core: 2. Of those that a mesh axis runs over, the one named last changes fastest.
Arguments:
- kohn_sham: bfloat16 [1536, 1536], P('qr', 'qc'), may hold values from -1 to 1, as said below
- pattern: int32 [24, 24], P('qr', 'qc'), may hold values from 0 to 1, as said below
- basis_centers: float32 [3, 1536], P(None, 'qr'), may hold values from 0 to 6.8
- occupations: float32 [1536], P('qr'), may hold values from 0.05 to 0.5
- atoms: float32 [4, 4, 4, 2, 1024], P(None, 'qr', 'qc', 'grp'), may hold values from -1.2 to 3.4, as said below
- neighbours: int32 [4, 4, 2, 2, 64, 1024], P('qr', 'qc', 'grp'), may hold values from 0 to 1023, as said below
- emb_atom: int32 [8192], P(('qr', 'qc', 'grp')), may hold values from 0 to 1023
- emb_dest: int32 [8192, 1], P(('qr', 'qc', 'grp')), may hold values from 0 to 3; in each aligned block of 256 rows (0 to 255, 256 to 511, ...) at most 96 rows name the same one
- emb_block: int32 [8192], P(('qr', 'qc', 'grp')), may hold values from 0 to 5
Outputs:
- sign_step: bfloat16 [1536, 1536], P(('qr', 'grp'), 'qc')
- forces: float32 [3, 4, 4, 2, 1024], P(None, 'qr', 'qc', 'grp')
Inputs may be any that keep to these rules, and one draw needn't show every extreme that they name: `kohn_sham`: zero outside the blocks that pattern marks. `pattern`: 1 on every diagonal block. `atoms`: rows 0 to 2 lie in the domain's box of edge 3.4; row 3 holds charges. `neighbours`: entry 0 of the fourth dimension is a slot, 0 to 26; entry 1 an atom of that domain. `emb_dest`: among the 256 records of one domain at most 96 name the same tile row.
All inputs are finite; a program needn't handle non-finite values.
Results may differ from a plain program's by a relative error of at most 0.012.
Values may be sent and summed in bfloat16 or wider, within the bound.
No kernel may reach another device: no remote copies, remote signals or barrier semaphores. Data moves between devices by JAX's collectives and lax.ppermute only.
A program may use at most 128 MiB of HBM per device.

v0:
```python
import jax
import jax.numpy as jnp
from jax import lax
from jax.sharding import PartitionSpec as P

BLOCK = 64
CAPACITY = 96


coulomb = 138.935
hartree_nm = 0.0529177
soften = 0.01
domain_edge = 3.4


def from_behind(value, axis, steps):
    count = lax.axis_size(axis)
    pairs = [(source, (source + steps) % count) for source in range(count)]
    return lax.ppermute(value, axis, pairs)


def padded(cells, sides, width):
    for axis, dim in sides:
        count = lax.axis_size(axis)
        head = lax.slice_in_dim(cells, 0, width, axis=dim)
        tail = lax.slice_in_dim(cells, cells.shape[dim] - width, cells.shape[dim], axis=dim)
        cells = jnp.concatenate(
            [
                lax.ppermute(tail, axis, [(i, (i + 1) % count) for i in range(count)]),
                cells,
                lax.ppermute(head, axis, [((i + 1) % count, i) for i in range(count)]),
            ],
            axis=dim,
        )
    return cells


def pair_terms(own_atoms, nearby, index_list):
    taken = nearby[:, index_list]
    offset = own_atoms[:3, None, :] - taken[:3]
    distance = jnp.sum(offset * offset, axis=0) + soften
    strength = coulomb * own_atoms[3][None, :] * taken[3] / (distance * jnp.sqrt(distance))
    return jnp.sum(offset * strength[None], axis=1)


def skew_columns(tile_piece, amount, extent):
    result = tile_piece
    for level_bit in range((extent - 1).bit_length()):
        arrived = from_behind(result, "qc", -(1 << level_bit))
        result = jnp.where(amount >> level_bit & 1 == 1, arrived, result)
    return result


def skew_rows(tile_piece, amount, extent):
    result = tile_piece
    for level_bit in range((extent - 1).bit_length()):
        arrived = from_behind(result, "qr", -(1 << level_bit))
        result = jnp.where(amount >> level_bit & 1 == 1, arrived, result)
    return result


def rotate_product(left_piece, right_piece, extent):

    def advance(turn, carried):
        summed, left_now, right_now = carried
        summed = summed + jnp.dot(left_now, right_now, preferred_element_type=jnp.float32)
        left_now = from_behind(left_now, "qc", -1)
        right_now = from_behind(right_now, "qr", -1)
        return (summed, left_now, right_now)

    initial = jnp.zeros((left_piece.shape[0], right_piece.shape[1]), jnp.float32)
    summed, left_now, right_now = lax.fori_loop(
        0, extent - 1, advance, (initial, left_piece, right_piece)
    )
    return summed + jnp.dot(left_now, right_now, preferred_element_type=jnp.float32)


def per_device(
    kohn_sham, pattern, basis_centers, occupations, atoms, neighbours, emb_atom, emb_dest, emb_block
):
    extent = lax.axis_size("qr")
    layers = lax.axis_size("grp")
    grid_row = lax.axis_index("qr")
    grid_column = lax.axis_index("qc")
    layer_index = lax.axis_index("grp")
    tile_order = kohn_sham.shape[0]
    slice_width = tile_order // layers
    tile_blocks = tile_order // BLOCK
    atom_count = atoms.shape[4]
    own_atoms = atoms[:, 0, 0, 0, :]
    anchor = jnp.stack([grid_row, grid_column, layer_index]).astype(jnp.float32) * domain_edge
    nearby = padded(atoms, (("qr", 1), ("qc", 2), ("grp", 3)), 1)
    places = jnp.arange(27, dtype=jnp.int32)
    displace = (
        jnp.stack([places // 9 - 1, places // 3 % 3 - 1, places % 3 - 1]).astype(jnp.float32)
        * domain_edge
    )
    grouped = nearby.reshape(4, 27, atom_count)
    located = grouped[:3] + displace[:, :, None]
    flat_near = jnp.concatenate([located, grouped[3:]], axis=0).reshape(4, 27 * atom_count)
    own_lists = neighbours[0, 0, 0]
    index_list = own_lists[0] * atom_count + own_lists[1]
    pair_force = pair_terms(own_atoms, flat_near, index_list)
    record_place = own_atoms[:3, emb_atom] + anchor[:, None]
    record_charge = own_atoms[3, emb_atom]
    target_row = emb_dest[:, 0]
    highest = lax.Precision.HIGHEST
    onehot = (target_row[:, None] == jnp.arange(extent, dtype=jnp.int32)[None, :]).astype(jnp.int32)
    ranking = jnp.sum((jnp.cumsum(onehot, axis=0) - 1) * onehot, axis=1)
    slot_index = target_row * CAPACITY + ranking
    records = jnp.concatenate([record_place, record_charge[None]], axis=0)
    buffer = (
        jnp.zeros((4, extent * CAPACITY), jnp.float32)
        .at[:, slot_index]
        .set(records)
        .reshape(4, extent, CAPACITY)
    )
    labels = (
        jnp.zeros((1, extent * CAPACITY), jnp.int32)
        .at[0, slot_index]
        .set(emb_block)
        .reshape(1, extent, CAPACITY)
    )
    centers = basis_centers.reshape(3, tile_blocks, BLOCK)
    weights = occupations.reshape(tile_blocks, BLOCK)
    received = lax.all_to_all(buffer, "qr", split_axis=1, concat_axis=1, tiled=True)
    block_labels = lax.all_to_all(labels, "qr", split_axis=1, concat_axis=1, tiled=True)
    chosen = (
        block_labels[0][:, :, None] == jnp.arange(tile_blocks, dtype=jnp.int32)[None, None, :]
    ).astype(jnp.float32)
    near_centers = jnp.einsum("xtb,nct->xncb", centers, chosen, precision=highest)
    near_weights = jnp.einsum("tb,nct->ncb", weights, chosen, precision=highest)
    offset = received[:3, :, :, None] - near_centers
    distance = jnp.sum(offset * offset, axis=0) + soften
    root_distance = jnp.sqrt(distance)
    potential_terms = hartree_nm * received[3][:, :, None] / root_distance
    pushes = (
        coulomb
        * received[3][None]
        * jnp.sum(near_weights[None] * offset / (distance * root_distance)[None], axis=3)
    )
    returned = lax.all_to_all(pushes, "qr", split_axis=1, concat_axis=1, tiled=True)
    returned, potential_terms, block_labels = (
        returned,
        jnp.transpose(potential_terms, (2, 0, 1)),
        block_labels,
    )
    chosen = (
        block_labels[0][:, :, None] == jnp.arange(tile_blocks, dtype=jnp.int32)[None, None, :]
    ).astype(jnp.float32)
    partial_field = jnp.einsum("bnc,nct->tb", potential_terms, chosen, precision=highest).reshape(
        tile_order
    )
    potential = lax.psum(partial_field, ("qc", "grp"))
    record_force = returned.reshape(3, extent * CAPACITY)[:, slot_index]
    embed_force = jnp.zeros((3, atom_count), jnp.float32).at[:, emb_atom].add(record_force)
    forces = (pair_force + embed_force).reshape(3, 1, 1, 1, atom_count)
    on_diagonal = (jnp.arange(tile_order)[:, None] == jnp.arange(tile_order)[None, :]) & (
        grid_row == grid_column
    )
    shifted = (
        kohn_sham.astype(jnp.float32) + jnp.where(on_diagonal, potential[:, None], 0.0)
    ).astype(jnp.bfloat16)
    keep_mask = jnp.repeat(jnp.repeat(pattern, BLOCK, axis=0), BLOCK, axis=1) == 1
    first_index = layer_index * slice_width
    left_slice = skew_columns(
        lax.dynamic_slice_in_dim(shifted, first_index, slice_width, 1), grid_row, extent
    )
    right_slice = skew_rows(
        lax.dynamic_slice_in_dim(shifted, first_index, slice_width, 0), grid_column, extent
    )
    square_part = jnp.where(keep_mask, rotate_product(left_slice, right_slice, extent), 0.0)
    square_whole = lax.psum(square_part.astype(jnp.bfloat16), "grp").astype(jnp.float32)
    square_rows = lax.dynamic_slice_in_dim(square_whole, first_index, slice_width, 0).astype(
        jnp.bfloat16
    )
    square_rows = skew_rows(square_rows, grid_column, extent)
    cube_part = jnp.where(keep_mask, rotate_product(left_slice, square_rows, extent), 0.0)
    cube_rows = lax.psum_scatter(
        cube_part.astype(jnp.bfloat16), "grp", scatter_dimension=0, tiled=True
    ).astype(jnp.float32)
    shifted_rows = lax.dynamic_slice_in_dim(shifted, first_index, slice_width, 0).astype(
        jnp.float32
    )
    sign_step = (0.5 * (3.0 * shifted_rows - cube_rows)).astype(jnp.bfloat16)
    return (sign_step, forces)


def solution(mesh):
    in_specs = (
        P("qr", "qc"),
        P("qr", "qc"),
        P(None, "qr"),
        P("qr"),
        P(None, "qr", "qc", "grp", None),
        P("qr", "qc", "grp", None, None, None),
        P(("qr", "qc", "grp")),
        P(("qr", "qc", "grp"), None),
        P(("qr", "qc", "grp")),
    )
    out_specs = (P(("qr", "grp"), "qc"), P(None, "qr", "qc", "grp", None))
    return jax.shard_map(
        per_device, mesh=mesh, in_specs=in_specs, out_specs=out_specs, check_vma=False
    )
```

profile of v0, /device:TPU:0, one launch (start us, length us, event | category | flops | bytes accessed | tf_op | source)
XLA Modules:
  0.0 918.6 jit_solution(8081175976852727858)
XLA Ops:
  7.2 3.1 collective-permute-start.10
  10.3 2.1 collective-permute-start.11
  16.7 1.6 scatter_custom_fusion
  18.9 3.2 all-to-all-start
  22.2 1.3 slice_multiply_fusion.1
  25.8 483.3 %while.31 = (s32[]{:T(128)}, f32[4,1024]{0,1:T(8,128)S(1)}, s32[256,2]{0,1:T(2,128)S(1)}, f32[256,3]{1,0:T(8,128)S(1)}, s32[]{:T(128)}, /*index=5*/s32[]{:T(128)}) while((s32[]{:T(128)}, f32[4,1024]{0,1:T(8,128)S(1)}, s32[256,2]{0,1:T(2,128)S(1)}, f32[256,3]{1,0:T(8,128)S(1)}, s32[]{:T(128)}, /*index=5*/s32[]{:T(128)}) %tuple.77), condition=%wide.while_cond, body=%wide.while_body.sunk | while | flops 2 | bytes 165 | solution.py:104
  28.3 1.3 dynamic-slice_bitcast_fusion.2
  30.2 1.3 dynamic-slice_bitcast_fusion.2
  32.0 1.3 dynamic-slice_bitcast_fusion.2
  33.9 1.3 dynamic-slice_bitcast_fusion.2
  35.8 1.3 dynamic-slice_bitcast_fusion.2
  37.7 1.3 dynamic-slice_bitcast_fusion.2
  39.6 1.3 dynamic-slice_bitcast_fusion.2
  41.5 1.3 dynamic-slice_bitcast_fusion.2
  43.4 1.3 dynamic-slice_bitcast_fusion.2
  45.3 1.3 dynamic-slice_bitcast_fusion.2
  47.1 1.3 dynamic-slice_bitcast_fusion.2
  49.0 1.3 dynamic-slice_bitcast_fusion.2
  50.9 1.3 dynamic-slice_bitcast_fusion.2
  52.8 1.3 dynamic-slice_bitcast_fusion.2
  54.7 1.3 dynamic-slice_bitcast_fusion.2
  56.6 1.3 dynamic-slice_bitcast_fusion.2
  58.5 1.3 dynamic-slice_bitcast_fusion.2
  60.4 1.3 dynamic-slice_bitcast_fusion.2
  64.1 1.3 dynamic-slice_bitcast_fusion.2
  66.0 1.3 dynamic-slice_bitcast_fusion.2
  67.9 1.3 dynamic-slice_bitcast_fusion.2
  509.1 2.0 gather_fusion
  516.2 5.1 all-to-all-start.1
  521.6 5.3 all-to-all-done.1
  527.6 13.6 %psum.14 = f32[384]{0:T(512)S(1)} all-reduce(f32[384]{0:T(512)S(1)} %reshape.297), channel_id=1, replica_groups=mesh['qr'=4,'qc'=4,'grp'=2] {'qc','grp'}, use_global_device_ids=true, to_apply=%region_6.7 | all-reduce | flops 384 | bytes 3072 | tf_op jit(solution)/shard_map/psum | solution.py:154
  544.4 3.2 all-to-all-start.2
  547.7 3.8 collective-permute-start.6
  552.2 1.9 collective-permute-done.6
  554.2 1.6 collective-permute-start.7
  555.8 1.5 collective-permute-done.5
  557.4 4.9 collective-permute-done.7
  562.3 23.4 %while.32 = (s32[]{:T(128)}, f32[384,384]{1,0:T(8,128)S(1)}, bf16[384,192]{1,0:T(8,128)(2,1)S(1)}, bf16[192,384]{1,0:T(8,128)(2,1)S(1)}, s32[]{:T(128)}, /*index=5*/s32[]{:T(128)}) while((s32[]{:T(128)}, f32[384,384]{1,0:T(8,128)S(1)}, bf16[384,192]{1,0:T(8,128)(2,1)S(1)}, bf16[192,384]{1,0:T(8,128)(2,1)S(1)}, s32[]{:T(128)}, ...), condition=%wide.region_8.9_spmd.clone, body=%wide.region_7.8_spmd.clone.sunk | while | flops 56918016 | bytes 3244191 | solution.py:72
  562.4 4.2 collective-permute-start.1
  567.0 2.3 collective-permute-done.1
  570.3 4.3 collective-permute-start.1
  575.0 2.5 collective-permute-done.1
  578.5 4.3 collective-permute-start.1
  583.2 2.5 collective-permute-done.1
  587.7 1.7 collective-permute-start.13
  589.4 22.8 %all-reduce.5.cloned.1.call-done = bf16[384,384]{1,0:T(8,128)(2,1)} async-done(((bf16[384,384]{1,0:T(8,128)(2,1)}), bf16[384,384]{1,0:T(8,128)(2,1)}) %all-reduce.5.cloned.1.call-update) | async-done | bytes 294928 | tf_op jit(solution)/shard_map/psum | solution.py:173
  613.1 3.4 collective-permute-start.8
  620.2 1.5 collective-permute-start.15
  622.8 3.4 collective-permute-done.14
  626.2 1.6 collective-permute-done.15
  630.3 22.9 %while.33 = (s32[]{:T(128)}, f32[384,384]{1,0:T(8,128)S(1)}, bf16[384,192]{1,0:T(8,128)(2,1)S(1)}, bf16[192,384]{1,0:T(8,128)(2,1)S(1)}, s32[]{:T(128)}, /*index=5*/s32[]{:T(128)}) while((s32[]{:T(128)}, f32[384,384]{1,0:T(8,128)S(1)}, bf16[384,192]{1,0:T(8,128)(2,1)S(1)}, bf16[192,384]{1,0:T(8,128)(2,1)S(1)}, s32[]{:T(128)}, ...), condition=%wide.region_11.12_spmd.clone, body=%wide.region_10.11_spmd.clone.sunk | while | flops 56918016 | bytes 3244191 | solution.py:72
  630.4 1.5 collective-permute-start.2
  631.9 2.3 collective-permute-start.3
  635.1 2.0 collective-permute-done.3
  637.1 1.3 collective-permute-start.2
  638.5 3.9 collective-permute-start.3
  642.8 2.3 collective-permute-done.3
  646.3 4.3 collective-permute-start.3
  651.0 2.3 collective-permute-done.3
  655.5 7.6 copy.39
  663.1 222.1 %gather_fusion.1 = f32[65536,4]{1,0:T(8,128)} fusion(f32[4,27648]{0,1:T(8,128)} %copy.39, s32[65536]{0:T(1024)S(1)} %broadcast_clamp_fusion), kind=kCustom, calls=%fused_computation.1 | custom fusion | bytes 2359296 | tf_op jit(solution)/shard_map/gather | solution.py:39
  885.2 19.5 %copy.40 = f32[64,1024,4]{1,0,2:T(8,128)S(1)} copy(f32[64,1024,4]{2,1,0:T(8,128)} %bitcast.103) | data formatting | bytes 2097152 | tf_op jit(solution)/shard_map/gather | solution.py:39
  905.3 4.1 scatter_custom_fusion.2
  910.2 1.6 multiply_convert_fusion
  (1139 shorter events, 492.9 us)
Async XLA Ops:
  7.2 579.7 %collective-permute-start.10 = (f32[4,1,1,1,1024]{4,3,2,1,0:T(1,128)}, f32[4,1,1,1,1024]{4,3,2,1,0:T(1,128)S(1)}, u32[]{:S(2)}, u32[]{:S(2)}) collective-permute-start(f32[4,1,1,1,1024]{4,3,2,1,0:T(1,128)} %param.17), channel_id=1, source_target_pairs={{0,8},{8,16},{16,24},{24,0},{1,9},{9,17},{17,25},{25,1},{2,10},{10... | collective-permute-start | bytes 49160 | tf_op jit(solution)/shard_map/ppermute | solution.py:29
  10.3 577.3 %collective-permute-start.11 = (f32[4,1,1,1,1024]{4,3,2,1,0:T(1,128)}, f32[4,1,1,1,1024]{4,3,2,1,0:T(1,128)S(1)}, u32[]{:S(2)}, u32[]{:S(2)}) collective-permute-start(f32[4,1,1,1,1024]{4,3,2,1,0:T(1,128)} %param.17), channel_id=1, source_target_pairs={{8,0},{16,8},{24,16},{0,24},{9,1},{17,9},{25,17},{1,25},{10,2},{18... | collective-permute-start | bytes 49160 | tf_op jit(solution)/shard_map/ppermute | solution.py:31
  13.0 498.8 %copy-start.2 = (s32[256]{0:T(256)}, s32[256]{0:T(256)S(1)}, u32[]{:S(2)}) copy-start(s32[256]{0:T(256)S(1)} %compare_select_fusion.2) | copy-start | bytes 3076
  18.9 497.3 %all-to-all-start = ((s32[1,4,96]{2,0,1:T(1,128)}), s32[1,4,96]{2,0,1:T(1,128)S(1)}, u32[]{:S(2)}, u32[]{:S(2)}) async-start(s32[1,4,96]{2,0,1:T(1,128)} %reshape.294), calls=%async_computation | async-start | bytes 4096 | tf_op jit(solution)/shard_map/all_to_all | solution.py:127
  516.2 10.7 %all-to-all-start.1 = ((f32[4,4,96]{2,0,1:T(4,128)}), f32[4,4,96]{2,0,1:T(4,128)S(1)}, u32[]{:S(2)}, u32[]{:S(2)}) async-start(f32[4,4,96]{2,0,1:T(4,128)} %copy.35), calls=%async_computation.1 | async-start | bytes 16384 | tf_op jit(solution)/shard_map/all_to_all | solution.py:126
  542.4 9.0 collective-permute-start.4
  544.4 74.3 %all-to-all-start.2 = ((f32[3,4,96]{2,0,1:T(4,128)}), f32[3,4,96]{2,0,1:T(4,128)S(1)}, u32[]{:S(2)}, u32[]{:S(2)}) async-start(f32[3,4,96]{2,0,1:T(4,128)} %broadcast_multiply_fusion), calls=%async_computation.3 | async-start | bytes 16384 | tf_op jit(solution)/shard_map/all_to_all | solution.py:142
  547.6 64.6 %all-reduce.5.cloned.1.call-start = ((), (), s32[]{:S(2)}) async-start(), calls=%async_computation.4 | async-start | bytes 589824 | tf_op jit(solution)/shard_map/psum | solution.py:173
  547.7 6.5 collective-permute-start.6
  551.6 5.7 collective-permute-start.5
  554.2 8.1 collective-permute-start.7
  562.3 4.7 collective-permute-start
  562.4 6.9 collective-permute-start.1
  569.3 5.7 collective-permute-start
  570.3 7.2 collective-permute-start.1
  577.5 5.7 collective-permute-start
  578.5 7.2 collective-permute-start.1
  586.8 323.4 %reduce-scatter.2.cloned.1.call-start = ((), (), s32[]{:S(2)}) async-start(), calls=%async_computation.5 | async-start | bytes 442368 | tf_op jit(solution)/shard_map/reduce_scatter | solution.py:179
  587.6 31.9 %collective-permute-start.12 = (f32[4,3,1,1,1024]{4,3,2,1,0:T(1,128)S(1)}, f32[4,3,1,1,1024]{4,3,2,1,0:T(1,128)S(1)}, u32[]{:S(2)}, u32[]{:S(2)}) collective-permute-start(f32[4,3,1,1,1024]{4,3,2,1,0:T(1,128)S(1)} %constant_dynamic-update-slice_fusion), channel_id=1, source_target_pairs={{0,2},{2,4},{4,6},{6,0},{1,3},{3,5},{5,7},{7,1},{8,10},{10,12},{12... | collective-permute-start | bytes 147464 | tf_op jit(solution)/shard_map/ppermute | solution.py:29
  587.7 31.8 %collective-permute-start.13 = (f32[4,3,1,1,1024]{4,3,2,1,0:T(1,128)S(1)}, f32[4,3,1,1,1024]{4,3,2,1,0:T(1,128)S(1)}, u32[]{:S(2)}, u32[]{:S(2)}) collective-permute-start(f32[4,3,1,1,1024]{4,3,2,1,0:T(1,128)S(1)} %constant_dynamic-update-slice_fusion), channel_id=1, source_target_pairs={{2,0},{4,2},{6,4},{0,6},{3,1},{5,3},{7,5},{1,7},{10,8},{12,10},{14... | collective-permute-start | bytes 147464 | tf_op jit(solution)/shard_map/ppermute | solution.py:31
  613.1 8.6 collective-permute-start.8
  619.6 6.5 collective-permute-start.14
  620.2 7.5 collective-permute-start.15
  622.7 7.6 collective-permute-start.9
  630.4 4.7 collective-permute-start.2
  631.9 5.2 collective-permute-start.3
  637.1 5.7 collective-permute-start.2
  638.5 6.6 collective-permute-start.3
  645.1 5.9 collective-permute-start.2
  646.3 7.0 collective-permute-start.3
  653.3 251.4 %copy-start = (f32[3,1,1,1,1024]{4,0,2,1,3:T(4,128)S(1)}, f32[3,1,1,1,1024]{4,0,2,1,3:T(4,128)}, u32[]{:S(2)}) copy-start(f32[3,1,1,1,1024]{4,0,2,1,3:T(4,128)} %copy.51) | copy-start | bytes 36868
  653.3 251.5 %copy-start.1 = (f32[1,1,1,1,1024]{4,3,2,1,0:T(1,128)S(1)}, f32[1,1,1,1,1024]{4,3,2,1,0:T(1,128)}, u32[]{:S(2)}) copy-start(f32[1,1,1,1,1024]{4,3,2,1,0:T(1,128)} %slice_multiply_fusion.1) | copy-start | bytes 12292
Sparse Core Ops, SparseCore 0:
  586.9 25.2 all-reduce.4
  654.5 13.4 reduce-scatter.1
where the time goes:
time: 935 us; the launch traced here: 919 us
  local copies, waits for them, and re-layouts  747 us (80%)
  starting transfers between devices  60.8 us (7%)
  waiting for transfers between devices  56.6 us (6%)
  other arithmetic  21.4 us (2%)
  between operations  14.4 us (2%)
  blocking collectives  13.6 us (1%)
    gather x1024, local copies, waits for them, and re-layouts  482 us
    gather x2, local copies, waits for them, and re-layouts, pair_terms(): taken = nearby[:, index_list]  242 us
    ppermute x18, starting transfers between devices, from_behind(): return lax.ppermute(value, axis, pairs)  40.1 us
    ppermute x18, waiting for transfers between devices, from_behind(): return lax.ppermute(value, axis, pairs)  23.5 us
    psum x1, waiting for transfers between devices, per_device(): lax.psum(square_part.astype(jnp.bfloat16), 'grp').astype(jnp.float32)  22.8 us
  transfers between devices with their start and end apart: 29, of which 15 were waited for; matrix products, arithmetic and copies ran while one was open for 84% of the time, Pallas kernels for 0%

commit v1 on v0

v1 whole, which is shorter than its diff:
```python
import functools

import jax
import jax.numpy as jnp
from jax import lax
from jax.experimental import pallas as pl
from jax.experimental.pallas import tpu as pltpu
from jax.sharding import PartitionSpec as P

BLOCK = 64
SUB, LANES = 8, 128

coulomb = 138.935
hartree_nm = 0.0529177
soften = 0.01
domain_edge = 3.4

ALL = ("qr", "qc", "grp")
VMEM = pltpu.MemorySpace.VMEM
SMEM = pltpu.MemorySpace.SMEM

LANE_PICK = lax.GatherDimensionNumbers(
    offset_dims=(),
    collapsed_slice_dims=(1,),
    start_index_map=(1,),
    operand_batching_dims=(0,),
    start_indices_batching_dims=(0,),
)


def pick_lanes(row, lane):
    return lax.gather(
        row, lane[..., None], LANE_PICK, (1, 1), mode=lax.GatherScatterMode.PROMISE_IN_BOUNDS
    )


def everyone(value, axes):
    count = 1
    for axis in (axes,) if isinstance(axes, str) else axes:
        count *= lax.axis_size(axis)
    copies = jnp.broadcast_to(value[None], (count,) + value.shape)
    return lax.all_to_all(copies, axes, split_axis=0, concat_axis=0, tiled=True)


def rotated(value, axis):
    count = lax.axis_size(axis)
    return [value] + [
        lax.ppermute(value, axis, [(i, (i + k) % count) for i in range(count)])
        for k in range(1, count)
    ]


def thirds(value):
    high = value.astype(jnp.bfloat16)
    rest = value - high.astype(jnp.float32)
    middle = rest.astype(jnp.bfloat16)
    low = (rest - middle.astype(jnp.float32)).astype(jnp.bfloat16)
    return high, middle, low


def records_kernel(
    anchor_ref, atoms_ref, pick_ref, block_ref, centers_ref, field_ref, force_ref
):
    atom_count = atoms_ref.shape[1]
    count = pick_ref.shape[1]
    blocks = centers_ref.shape[1]
    one_atom = (
        lax.broadcasted_iota(jnp.int32, (atom_count, count), 0) == pick_ref[...]
    ).astype(jnp.bfloat16)
    one_block = (
        lax.broadcasted_iota(jnp.int32, (blocks, count), 0) == block_ref[...]
    ).astype(jnp.bfloat16)

    def chosen_atoms(rows):
        pieces = [
            jnp.dot(piece, one_atom, preferred_element_type=jnp.float32) for piece in thirds(rows)
        ]
        return pieces[0] + pieces[1] + pieces[2]

    def chosen_centers(rows):
        pieces = [
            lax.dot_general(
                piece, one_block, (((0,), (0,)), ((), ())), preferred_element_type=jnp.float32
            )
            for piece in thirds(rows)
        ]
        return pieces[0] + pieces[1] + pieces[2]

    taken = chosen_atoms(atoms_ref[...])
    charge = taken[3:4]
    offset = [taken[c : c + 1] + anchor_ref[0, c] - chosen_centers(centers_ref[c]) for c in range(3)]
    weight = chosen_centers(centers_ref[3])
    distance = offset[0] * offset[0] + offset[1] * offset[1] + offset[2] * offset[2] + soften
    inverse = lax.rsqrt(distance)
    terms = hartree_nm * charge * inverse
    partial = jnp.zeros((blocks, BLOCK), jnp.float32)
    for piece in thirds(terms):
        partial = partial + lax.dot_general(
            one_block, piece, (((1,), (1,)), ((), ())), preferred_element_type=jnp.float32
        )
    field_ref[...] = partial
    strength = weight * (inverse * inverse * inverse)
    pushes = [
        coulomb * charge * jnp.sum(strength * offset[c], axis=0, keepdims=True) for c in range(3)
    ]
    pushes = jnp.concatenate(pushes + [jnp.zeros((5, count), jnp.float32)], axis=0)
    total = jnp.zeros((8, atom_count), jnp.float32)
    for piece in thirds(pushes):
        total = total + lax.dot_general(
            piece, one_atom, (((1,), (1,)), ((), ())), preferred_element_type=jnp.float32
        )
    force_ref[...] = total


def embedding(anchor, own, pick, block, centers):
    atom_count, count, blocks = own.shape[1], pick.shape[1], centers.shape[1]
    return pl.pallas_call(
        records_kernel,
        out_shape=(
            jax.ShapeDtypeStruct((blocks, BLOCK), jnp.float32),
            jax.ShapeDtypeStruct((8, atom_count), jnp.float32),
        ),
        in_specs=[pl.BlockSpec(memory_space=SMEM)] + [pl.BlockSpec(memory_space=VMEM)] * 4,
        out_specs=(pl.BlockSpec(memory_space=VMEM),) * 2,
        cost_estimate=pl.CostEstimate(flops=10**9, bytes_accessed=10**6, transcendentals=0),
        name="embedding",
    )(anchor, own, pick, block, centers)


def packing_kernel(ids_ref, near_ref, packed_ref, scale_ref):
    domains = packed_ref.shape[1] // SUB
    low = [near_ref[ids_ref[0], c] for c in range(4)]
    high = list(low)
    for d in range(1, domains):
        for c in range(4):
            value = near_ref[ids_ref[d], c]
            low[c] = jnp.minimum(low[c], value)
            high[c] = jnp.maximum(high[c], value)
    steps = 65535.0
    base, back, step = [], [], []
    for c in range(4):
        least = jnp.min(low[c], axis=(0, 1), keepdims=True)
        width = jnp.maximum(jnp.max(high[c], axis=(0, 1), keepdims=True) - least, 1e-30)
        base.append(jnp.broadcast_to(least, (SUB, LANES)))
        back.append(jnp.broadcast_to(steps / width, (SUB, LANES)))
        step.append(jnp.broadcast_to(width * (1.0 / steps), (SUB, LANES)))
        scale_ref[c] = base[c]
        scale_ref[4 + c] = step[c]
    for d in range(domains):
        code = [
            jnp.clip((near_ref[ids_ref[d], c] - base[c]) * back[c] + 0.5, 0.0, steps).astype(
                jnp.int32
            )
            for c in range(4)
        ]
        packed_ref[0, d * SUB : (d + 1) * SUB, :] = code[0] | (code[1] << 16)
        packed_ref[1, d * SUB : (d + 1) * SUB, :] = code[2] | (code[3] << 16)


def packing(ids, near):
    domains = ids.shape[0]
    return pl.pallas_call(
        packing_kernel,
        out_shape=(
            jax.ShapeDtypeStruct((2, domains * SUB, LANES), jnp.int32),
            jax.ShapeDtypeStruct((8, SUB, LANES), jnp.float32),
        ),
        in_specs=[pl.BlockSpec(memory_space=SMEM), pl.BlockSpec(memory_space=VMEM)],
        out_specs=(pl.BlockSpec(memory_space=VMEM),) * 2,
        cost_estimate=pl.CostEstimate(flops=10**7, bytes_accessed=10**6, transcendentals=0),
        name="packing",
    )(ids, near)


def compact(place, count):
    if count >= 3:
        return place
    if count == 2:
        return jnp.where(place == 1, 0, 1)
    return jnp.zeros_like(place)


def pair_kernel(counts, first, groups, lists_ref, own_ref, packed_ref, scale_ref, force_ref):
    rows = packed_ref.shape[1]
    parts = lists_ref.shape[1] // SUB
    distinct = [min(3, count) for count in counts]

    def group(a, _):
        column = pl.multiple_of((first + a) * LANES, LANES)
        mine = [
            jnp.broadcast_to(own_ref[c, pl.ds(first + a, 1), :], (SUB, LANES)) for c in range(4)
        ]

        def part(b, sums):
            start = pl.multiple_of(b * SUB, SUB)
            slot = lists_ref[0, pl.ds(start, SUB), pl.ds(column, LANES)]
            member = lists_ref[1, pl.ds(start, SUB), pl.ds(column, LANES)]
            p = (slot * 57) >> 9
            rest = slot - 9 * p
            q = (rest * 11) >> 5
            r = rest - 3 * q
            domain = (
                compact(p, counts[0]) * distinct[1] + compact(q, counts[1])
            ) * distinct[2] + compact(r, counts[2])
            row = domain * SUB + (member >> 7)
            lane = member & (LANES - 1)
            words = [jnp.zeros((SUB, LANES), jnp.int32) for _ in range(2)]
            for k in range(rows):
                here = row == k
                for w in range(2):
                    line = jnp.broadcast_to(packed_ref[w, k : k + 1, :], (SUB, LANES))
                    words[w] = jnp.where(here, pick_lanes(line, lane), words[w])
            code = [
                words[0] & 0xFFFF,
                (words[0] >> 16) & 0xFFFF,
                words[1] & 0xFFFF,
                (words[1] >> 16) & 0xFFFF,
            ]
            value = [code[c].astype(jnp.float32) * scale_ref[4 + c] + scale_ref[c] for c in range(4)]
            shift = [(place - 1).astype(jnp.float32) * domain_edge for place in (p, q, r)]
            offset = [mine[c] - (value[c] + shift[c]) for c in range(3)]
            distance = (
                offset[0] * offset[0] + offset[1] * offset[1] + offset[2] * offset[2] + soften
            )
            inverse = lax.rsqrt(distance)
            strength = value[3] * (inverse * inverse * inverse)
            return tuple(sums[c] + offset[c] * strength for c in range(3))

        zero = jnp.zeros((SUB, LANES), jnp.float32)
        sums = lax.fori_loop(0, parts, part, (zero, zero, zero))
        for c in range(3):
            force_ref[c, pl.ds(a, 1), :] = (
                coulomb * mine[3][:1] * jnp.sum(sums[c], axis=0, keepdims=True)
            )
        return 0

    lax.fori_loop(0, groups, group, 0)


def pair_forces(counts, first, groups, lists, own, packed, scale):
    return pl.pallas_call(
        functools.partial(pair_kernel, counts, first, groups),
        out_shape=jax.ShapeDtypeStruct((3, groups, LANES), jnp.float32),
        in_specs=[pl.BlockSpec(memory_space=VMEM)] * 4,
        out_specs=pl.BlockSpec(memory_space=VMEM),
        cost_estimate=pl.CostEstimate(
            flops=10**8 * groups, bytes_accessed=10**6, transcendentals=0
        ),
        name="pairs",
    )(lists, own, packed, scale)


def neighbourhood(block):
    counts = tuple(lax.axis_size(axis) for axis in ALL)
    here = [lax.axis_index(axis) for axis in ALL]
    reach = []
    for count in counts:
        reach.append((-1, 0, 1) if count >= 3 else (0, 1) if count == 2 else (0,))
    total = counts[0] * counts[1] * counts[2]
    if total <= 64:
        near = everyone(block, ALL)
        ids = [
            (((here[0] + i) % counts[0]) * counts[1] + (here[1] + j) % counts[1]) * counts[2]
            + (here[2] + k) % counts[2]
            for i in reach[0]
            for j in reach[1]
            for k in reach[2]
        ]
        return near, jnp.stack(ids).astype(jnp.int32)
    near = block[None]
    for axis, count in reversed(tuple(zip(ALL, counts))):
        ahead = [((i + 1) % count, i) for i in range(count)]
        behind = [(i, (i + 1) % count) for i in range(count)]
        if count >= 3:
            near = jnp.concatenate(
                [lax.ppermute(near, axis, behind), near, lax.ppermute(near, axis, ahead)], axis=0
            )
        elif count == 2:
            near = jnp.concatenate([near, lax.ppermute(near, axis, ahead)], axis=0)
    return near, jnp.arange(near.shape[0], dtype=jnp.int32)


def per_device(
    kohn_sham, pattern, basis_centers, occupations, atoms, neighbours, emb_atom, emb_dest, emb_block
):
    counts = tuple(lax.axis_size(axis) for axis in ALL)
    extent, layers = counts[0], counts[2]
    grid_row = lax.axis_index("qr")
    grid_column = lax.axis_index("qc")
    layer = lax.axis_index("grp")
    order = kohn_sham.shape[0]
    width = order // layers
    tile_blocks = order // BLOCK
    atom_count = atoms.shape[4]
    record_count = emb_atom.shape[0]

    basis = jnp.concatenate([basis_centers, occupations[None]], axis=0)
    basis_all = everyone(basis, "qr")
    centers = (
        jnp.transpose(basis_all.reshape(extent, 4, tile_blocks, BLOCK), (1, 0, 2, 3))
    ).reshape(4, extent * tile_blocks, BLOCK)

    first = layer * width
    left_own = lax.dynamic_slice_in_dim(kohn_sham, first, width, 1)
    right_own = lax.dynamic_slice_in_dim(kohn_sham, first, width, 0)
    left = everyone(left_own, "qc")
    rights = rotated(right_own, "qr")

    near, ids = neighbourhood(atoms.reshape(4, SUB, atom_count // SUB))

    anchor = (
        jnp.stack([grid_row, grid_column, layer]).astype(jnp.float32)[None] * domain_edge
    )
    field, embed_force = embedding(
        anchor,
        atoms.reshape(4, atom_count),
        emb_atom[None],
        (emb_dest[:, 0] * tile_blocks + emb_block)[None],
        centers,
    )
    field_all = everyone(field.reshape(extent * order), ALL)
    potential = jnp.sum(field_all, axis=0).reshape(extent, order)

    keep = jnp.repeat(jnp.repeat(pattern, BLOCK, axis=0), BLOCK, axis=1) == 1
    behind = [(grid_row - k) % extent for k in range(extent)]
    lefts = [lax.dynamic_index_in_dim(left, tile, 0, keepdims=False) for tile in behind]

    def swap_layers(part):
        wide = part.reshape(layers, width, order)
        mine = lax.dynamic_index_in_dim(wide, layer, 0, keepdims=False)
        got = lax.all_to_all(
            wide.astype(jnp.bfloat16), "grp", split_axis=0, concat_axis=0, tiled=True
        )
        other = jnp.arange(layers)[:, None, None] != layer
        return mine + jnp.sum(jnp.where(other, got.astype(jnp.float32), 0.0), axis=0)

    product = jnp.zeros((order, order), jnp.float32)
    for k in range(extent):
        product = product + jnp.dot(lefts[k], rights[k], preferred_element_type=jnp.float32)
    product = jnp.where(keep, product, 0.0)
    product_rows = swap_layers(product).astype(jnp.bfloat16)
    products = rotated(product_rows, "qr")

    own_column = lax.dynamic_index_in_dim(potential, grid_column, 0, keepdims=False)
    rows_at = jnp.arange(width)[:, None] + first
    columns_at = jnp.arange(order)[None, :]
    cube = jnp.zeros((order, order), jnp.float32)
    for k in range(extent):
        tile = behind[k]
        row_field = lax.dynamic_slice_in_dim(
            lax.dynamic_index_in_dim(potential, tile, 0, keepdims=False), first, width, 0
        )
        matrix = rights[k].astype(jnp.float32)
        diagonal = (rows_at == columns_at) & (tile == grid_column)
        square = (
            products[k].astype(jnp.float32)
            + matrix * (row_field[:, None] + own_column[None, :])
            + jnp.where(diagonal, row_field[:, None] * row_field[:, None], 0.0)
        ).astype(jnp.bfloat16)
        operand = lefts[k]
        if k == 0:
            on_diagonal = jnp.arange(order)[:, None] == jnp.arange(width)[None, :] + first
            operand = (
                operand.astype(jnp.float32) + jnp.where(on_diagonal, row_field[None, :], 0.0)
            ).astype(jnp.bfloat16)
        cube = cube + jnp.dot(operand, square, preferred_element_type=jnp.float32)
    cube = jnp.where(keep, cube, 0.0)
    cube_rows = swap_layers(cube)
    row_field = lax.dynamic_slice_in_dim(
        lax.dynamic_index_in_dim(potential, grid_row, 0, keepdims=False), first, width, 0
    )
    diagonal = (rows_at == columns_at) & (grid_row == grid_column)
    shifted = (
        right_own.astype(jnp.float32) + jnp.where(diagonal, row_field[:, None], 0.0)
    ).astype(jnp.bfloat16)
    sign_step = (0.5 * (3.0 * shifted.astype(jnp.float32) - cube_rows)).astype(jnp.bfloat16)

    own = atoms.reshape(4, SUB, atom_count // SUB)
    packed, scale = packing(ids, near)
    lists = neighbours[0, 0, 0]
    pieces = 4
    groups = SUB // pieces
    pair_force = jnp.concatenate(
        [
            pair_forces(counts, i * groups, groups, lists, own, packed, scale)
            for i in range(pieces)
        ],
        axis=1,
    )
    forces = pair_force.reshape(3, atom_count) + embed_force[:3]
    return (sign_step, forces.reshape(3, 1, 1, 1, atom_count))


def solution(mesh):
    in_specs = (
        P("qr", "qc"),
        P("qr", "qc"),
        P(None, "qr"),
        P("qr"),
        P(None, "qr", "qc", "grp", None),
        P("qr", "qc", "grp", None, None, None),
        P(("qr", "qc", "grp")),
        P(("qr", "qc", "grp"), None),
        P(("qr", "qc", "grp")),
    )
    out_specs = (P(("qr", "grp"), "qc"), P(None, "qr", "qc", "grp", None))
    return jax.shard_map(
        per_device, mesh=mesh, in_specs=in_specs, out_specs=out_specs, check_vma=False
    )
```

time: 935 us -> 137 us (0.15); the launches traced: 919 us -> 135 us
  local copies, waits for them, and re-layouts: 747 us -> 10.5 us
  Pallas kernels: 0 us -> 36.8 us
  starting transfers between devices: 60.8 us -> 29.4 us
  other arithmetic: 21.4 us -> 4.08 us
  waiting for transfers between devices: 56.6 us -> 42.5 us
  between operations: 14.4 us -> 1.18 us
    gather x1028 -> x0, local copies, waits for them, and re-layouts: 726 us -> none
    ppermute x24 -> x6, starting transfers between devices: 49.1 us -> 10 us  [rotated(): lax.ppermute(value, axis, [(i, (i + k) % count) for i in range(count)])]
    pallas_call x0 -> x6, Pallas kernels: none -> 36.8 us  [the longest x4 32.2 us: pair_forces(): pl.pallas_call(functools.partial(pair_kernel, counts, first, groups), out...]
    all_to_all x3 -> x5, waiting for transfers between devices: 5.34 us -> 34.2 us  [the longest x4 28.8 us: everyone(): return lax.all_to_all(copies, axes, split_axis=0, concat_axis=0, tiled=True)]
    psum x1 -> x0, waiting for transfers between devices: 22.8 us -> none  [per_device(): lax.psum(square_part.astype(jnp.bfloat16), 'grp').astype(jnp.float32)]
    ppermute x24 -> x6, waiting for transfers between devices: 28.5 us -> 8.25 us  [rotated(): lax.ppermute(value, axis, [(i, (i + k) % count) for i in range(count)])]
    psum x1 -> x0, blocking collectives: 13.6 us -> none  [per_device(): potential = lax.psum(partial_field, ('qc', 'grp'))]
    all_to_all x3 -> x5, starting transfers between devices: 11.6 us -> 19.4 us  [the longest x4 15.9 us: everyone(): return lax.all_to_all(copies, axes, split_axis=0, concat_axis=0, tiled=True)]
  transfers between devices with their start and end apart: 29 -> 11, of which waited for: 15 -> 7; matrix products, arithmetic and copies ran while one was open for 84% -> 9% of each run, Pallas kernels for 0% -> 2%
where the time goes in v1:
time: 137 us; the launch traced here: 135 us
  waiting for transfers between devices  42.5 us (31%)
  Pallas kernels  36.8 us (27%)
  starting transfers between devices  29.4 us (21%)
  local copies, waits for them, and re-layouts  10.5 us (8%)
  blocking collectives  8.03 us (6%)
  other arithmetic  4.08 us (3%)
  matrix products  2.92 us (2%)
    pallas_call x4, Pallas kernels, pair_forces(): pl.pallas_call(functools.partial(pair_kernel, counts, first, groups), out...  32.2 us
    all_to_all x4, waiting for transfers between devices, everyone(): return lax.all_to_all(copies, axes, split_axis=0, concat_axis=0, tiled=True)  28.8 us
    all_to_all x4, starting transfers between devices, everyone(): return lax.all_to_all(copies, axes, split_axis=0, concat_axis=0, tiled=True)  15.9 us
    ppermute x6, starting transfers between devices, rotated(): lax.ppermute(value, axis, [(i, (i + k) % count) for i in range(count)])  10 us
    ppermute x6, waiting for transfers between devices, rotated(): lax.ppermute(value, axis, [(i, (i + k) % count) for i in range(count)])  8.25 us
    all_to_all x1, blocking collectives, swap_layers(): lax.all_to_all(wide.astype(jnp.bfloat16), 'grp', split_axis=0, concat_axi...  8.03 us
    all_to_all x1, waiting for transfers between devices, swap_layers(): lax.all_to_all(wide.astype(jnp.bfloat16), 'grp', split_axis=0, concat_axi...  5.44 us
    broadcast_in_dim x5, local copies, waits for them, and re-layouts, everyone(): copies = jnp.broadcast_to(value[None], (count,) + value.shape)  3.89 us
  transfers between devices with their start and end apart: 11, of which 7 were waited for; matrix products, arithmetic and copies ran while one was open for 9% of the time, Pallas kernels for 2%

profile of v1, /device:TPU:0, one launch (start us, length us, event | category | flops | bytes accessed | tf_op | source)
XLA Modules:
  0.0 135.3 jit_solution(3771556236510492092)
XLA Ops:
  0.7 1.0 constant_dynamic-slice_fusion.2
  1.6 5.1 %collective-permute-start.2 = (bf16[192,384]{1,0:T(8,128)(2,1)S(1)}, bf16[192,384]{1,0:T(8,128)(2,1)S(1)}, u32[]{:S(2)}, u32[]{:S(2)}) collective-permute-start(bf16[192,384]{1,0:T(8,128)(2,1)S(1)} %constant_dynamic-slice_fusion.2), channel_id=1, source_target_pairs={{0,24},{8,0},{16,8},{24,16},{1,25},{9,1},{17,9},{25,17},{2,26},{10... | collective-permute-start | bytes 442376 | tf_op jit(solution)/shard_map/ppermute | solution.py:48
  6.8 1.0 collective-permute-start.1
  7.8 0.6 broadcast_in_dim.140
  8.4 4.8 %all-to-all-start = ((f32[4,4,384]{2,1,0:T(4,128)}), f32[4,4,384]{2,1,0:T(4,128)S(1)}, u32[]{:S(2)}, u32[]{:S(2)}) async-start(f32[4,4,384]{2,1,0:T(4,128)} %broadcast_in_dim.140), calls=%async_computation | async-start | bytes 49152 | tf_op jit(solution)/shard_map/all_to_all | solution.py:42
  13.2 0.1 constant_dynamic-slice_fusion.1
  13.4 0.1 copy.35
  13.5 0.1 broadcast_in_dim.146
  13.6 0.1 eq.148
  13.8 0.2 copy.38
  14.0 0.0 copy-start.2
  14.0 0.1 copy.36
  14.2 0.6 copy-done.2
  14.7 0.6 copy.45
  15.3 4.5 %all-to-all-done = f32[4,4,384]{2,1,0:T(4,128)S(1)} async-done(((f32[4,4,384]{2,1,0:T(4,128)}), f32[4,4,384]{2,1,0:T(4,128)S(1)}, u32[]{:S(2)}, u32[]{:S(2)}) %all-to-all-start) | async-done | bytes 24608 | tf_op jit(solution)/shard_map/all_to_all | solution.py:42
  19.8 0.9 broadcast_in_dim.148
  20.7 3.6 %all-to-all-start.2 = ((bf16[4,384,192]{1,2,0:T(8,128)(2,1)}), bf16[4,384,192]{1,2,0:T(8,128)(2,1)S(1)}, u32[]{:S(2)}, u32[]{:S(2)}) async-start(bf16[4,384,192]{1,2,0:T(8,128)(2,1)} %broadcast_in_dim.148), calls=%async_computation.2 | async-start | bytes 1179648 | tf_op jit(solution)/shard_map/all_to_all | solution.py:42
  24.3 0.0 copy-start.10
  24.3 0.7 copy-done.10
  25.0 0.6 add.396
  25.6 0.7 fusion.73.anchor_ref
  26.3 0.1 reshape.159
  26.4 0.6 copy.33.centers_ref
  27.0 2.7 %embedding.1 = (f32[24,64]{1,0:T(8,128)}, f32[8,1024]{1,0:T(8,128)}) custom-call(f32[1,3]{1,0:T(1,128)} %fusion.73.anchor_ref, f32[4,1024]{1,0:T(4,128)} %bitcast.108, s32[1,256]{1,0:T(1,128)} %bitcast.119, s32[1,256]{1,0:T(1,128)} %bitcast.114, f32[4,24,64]{2,1,0:T(8,128)} %copy.33.centers_ref), custom_call_target="tpu_custom_call" | custom-call | flops 1000000000 | bytes 1000000 | tf_op jit(solution)/shard_map/embedding/pallas_call | solution.py:117
  29.7 0.8 broadcast_in_dim.141
  30.4 3.4 %all-to-all-done.2 = bf16[4,384,192]{1,2,0:T(8,128)(2,1)S(1)} async-done(((bf16[4,384,192]{1,2,0:T(8,128)(2,1)}), bf16[4,384,192]{1,2,0:T(8,128)(2,1)S(1)}, u32[]{:S(2)}, u32[]{:S(2)}) %all-to-all-start.2) | async-done | bytes 589856 | tf_op jit(solution)/shard_map/all_to_all | solution.py:42
  33.8 0.8 broadcast_in_dim.142
  34.6 3.9 %all-to-all-start.1 = ((f32[32,1,1536]{2,1,0:T(1,128)}), f32[32,1,1536]{2,1,0:T(1,128)S(1)}, u32[]{:S(2)}, u32[]{:S(2)}) async-start(f32[32,1,1536]{2,1,0:T(1,128)} %broadcast_in_dim.142), calls=%async_computation.1 | async-start | bytes 393216 | tf_op jit(solution)/shard_map/all_to_all | solution.py:42
  38.5 0.3 fusion.25
  38.8 0.3 convolution_add_fusion.4
  39.1 0.3 fusion.19
  39.4 0.0 collective-permute-done.1
  39.4 0.3 fusion.2
  39.7 0.7 convert_element_type.83
  40.5 7.7 %all-to-all-done.1 = f32[32,1,1536]{2,1,0:T(1,128)S(1)} async-done(((f32[32,1,1536]{2,1,0:T(1,128)}), f32[32,1,1536]{2,1,0:T(1,128)S(1)}, u32[]{:S(2)}, u32[]{:S(2)}) %all-to-all-start.1) | async-done | bytes 196640 | tf_op jit(solution)/shard_map/all_to_all | solution.py:42
  48.1 3.4 %all-to-all-start.3 = ((bf16[2,192,384]{2,1,0:T(8,128)(2,1)}), bf16[2,192,384]{2,1,0:T(8,128)(2,1)S(1)}, u32[]{:S(2)}, u32[]{:S(2)}) async-start(bf16[2,192,384]{2,1,0:T(8,128)(2,1)} %convert_element_type.83), calls=%async_computation.3 | async-start | bytes 589824 | tf_op jit(solution)/shard_map/all_to_all | solution.py:331
  51.6 0.1 reduce_sum.27
  51.8 0.1 fusion.78
  52.0 5.4 %all-to-all-done.3 = bf16[2,192,384]{2,1,0:T(8,128)(2,1)S(1)} async-done(((bf16[2,192,384]{2,1,0:T(8,128)(2,1)}), bf16[2,192,384]{2,1,0:T(8,128)(2,1)S(1)}, u32[]{:S(2)}, u32[]{:S(2)}) %all-to-all-start.3) | async-done | bytes 294944 | tf_op jit(solution)/shard_map/all_to_all | solution.py:331
  57.4 0.1 select_reduce_fusion.1
  57.6 0.1 collective-permute-start.3
  57.7 1.9 %collective-permute-start.4 = (bf16[192,384]{1,0:T(8,128)(2,1)S(1)}, bf16[192,384]{1,0:T(8,128)(2,1)S(1)}, u32[]{:S(2)}, u32[]{:S(2)}) collective-permute-start(bf16[192,384]{1,0:T(8,128)(2,1)S(1)} %fusion.10), channel_id=1, source_target_pairs={{0,16},{8,24},{16,0},{24,8},{1,17},{9,25},{17,1},{25,9},{2,18},{10... | collective-permute-start | bytes 442376 | tf_op jit(solution)/shard_map/ppermute | solution.py:48
  59.5 2.0 %collective-permute-start.5 = (bf16[192,384]{1,0:T(8,128)(2,1)S(1)}, bf16[192,384]{1,0:T(8,128)(2,1)S(1)}, u32[]{:S(2)}, u32[]{:S(2)}) collective-permute-start(bf16[192,384]{1,0:T(8,128)(2,1)S(1)} %fusion.10), channel_id=1, source_target_pairs={{0,24},{8,0},{16,8},{24,16},{1,25},{9,1},{17,9},{25,17},{2,26},{10... | collective-permute-start | bytes 442376 | tf_op jit(solution)/shard_map/ppermute | solution.py:48
  61.5 0.5 fusion.16
  61.9 4.2 %collective-permute-done.3 = bf16[192,384]{1,0:T(8,128)(2,1)S(1)} collective-permute-done((bf16[192,384]{1,0:T(8,128)(2,1)S(1)}, bf16[192,384]{1,0:T(8,128)(2,1)S(1)}, u32[]{:S(2)}, u32[]{:S(2)}) %collective-permute-start.3) | collective-permute-done | bytes 147488 | tf_op jit(solution)/shard_map/ppermute | solution.py:48
  66.2 0.4 convolution_add_fusion.2
  66.6 4.0 %collective-permute-done.4 = bf16[192,384]{1,0:T(8,128)(2,1)S(1)} collective-permute-done((bf16[192,384]{1,0:T(8,128)(2,1)S(1)}, bf16[192,384]{1,0:T(8,128)(2,1)S(1)}, u32[]{:S(2)}, u32[]{:S(2)}) %collective-permute-start.4) | collective-permute-done | bytes 147488 | tf_op jit(solution)/shard_map/ppermute | solution.py:48
  70.6 0.4 convolution_add_fusion.1
  71.1 0.4 fusion
  71.5 8.0 %all_to_all.31 = bf16[2,192,384]{2,1,0:T(8,128)(2,1)S(1)} all-to-all(bf16[2,192,384]{2,1,0:T(8,128)(2,1)S(1)} %convert_element_type.97), channel_id=1, replica_groups=mesh['qr'=4,'qc'=4,'grp'=2] {'grp'}, dimensions={0} | all-to-all | bytes 589824 | tf_op jit(solution)/shard_map/all_to_all | solution.py:331
  79.6 0.9 broadcast_in_dim.159
  80.4 3.6 %all-to-all-start.5 = ((f32[32,4,8,128]{3,2,1,0:T(8,128)}), f32[32,4,8,128]{3,2,1,0:T(8,128)S(1)}, u32[]{:S(2)}, u32[]{:S(2)}) async-start(f32[32,4,8,128]{3,2,1,0:T(8,128)} %broadcast_in_dim.159), calls=%async_computation.5 | async-start | bytes 1048576 | tf_op jit(solution)/shard_map/all_to_all | solution.py:42
  84.2 0.6 stack.91.ids_ref
  84.8 0.1 select_reduce_fusion
  84.9 0.9 fusion.9
  85.8 13.2 %all-to-all-done.5.near_ref = f32[32,4,8,128]{3,2,1,0:T(8,128)S(1)} async-done(((f32[32,4,8,128]{3,2,1,0:T(8,128)}), f32[32,4,8,128]{3,2,1,0:T(8,128)S(1)}, u32[]{:S(2)}, u32[]{:S(2)}) %all-to-all-start.5) | async-done | bytes 524320 | tf_op jit(solution)/shard_map/all_to_all | solution.py:42
  99.0 0.8 copy-done
  99.8 1.9 %packing.1 = (s32[2,144,128]{2,1,0:T(8,128)}, f32[8,8,128]{2,1,0:T(8,128)}) custom-call(s32[18]{0:T(128)} %stack.91.ids_ref, f32[32,4,8,128]{3,2,1,0:T(8,128)} %copy-done), custom_call_target="tpu_custom_call" | custom-call | flops 10000000 | bytes 1000000 | tf_op jit(solution)/shard_map/packing/pallas_call | solution.py:162
  101.8 8.0 %pairs.7 = f32[3,2,128]{2,1,0:T(2,128)} custom-call(s32[2,64,1024]{2,1,0:T(8,128)} %bitcast.115, f32[4,8,128]{2,1,0:T(8,128)} %bitcast.94, s32[2,144,128]{2,1,0:T(8,128)} %get-tuple-element.7.packed_ref, f32[8,8,128]{2,1,0:T(8,128)} %get-tuple-element.8.scale_ref), custom_call_target="tpu_custom_call" | custom-call | flops 200000000 | bytes 1000000 | tf_op jit(solution)/shard_map/pairs/pallas_call | solution.py:241
  109.8 8.0 %pairs.6 = f32[3,2,128]{2,1,0:T(2,128)} custom-call(s32[2,64,1024]{2,1,0:T(8,128)} %bitcast.116, f32[4,8,128]{2,1,0:T(8,128)} %bitcast.95, s32[2,144,128]{2,1,0:T(8,128)} %get-tuple-element.7.packed_ref, f32[8,8,128]{2,1,0:T(8,128)} %get-tuple-element.8.scale_ref), custom_call_target="tpu_custom_call" | custom-call | flops 200000000 | bytes 1000000 | tf_op jit(solution)/shard_map/pairs/pallas_call | solution.py:241
  117.9 8.0 %pairs.5 = f32[3,2,128]{2,1,0:T(2,128)} custom-call(s32[2,64,1024]{2,1,0:T(8,128)} %bitcast.117, f32[4,8,128]{2,1,0:T(8,128)} %bitcast.96, s32[2,144,128]{2,1,0:T(8,128)} %get-tuple-element.7.packed_ref, f32[8,8,128]{2,1,0:T(8,128)} %get-tuple-element.8.scale_ref), custom_call_target="tpu_custom_call" | custom-call | flops 200000000 | bytes 1000000 | tf_op jit(solution)/shard_map/pairs/pallas_call | solution.py:241
  125.9 8.1 %pairs.4 = f32[3,2,128]{2,1,0:T(2,128)} custom-call(s32[2,64,1024]{2,1,0:T(8,128)} %bitcast.118, f32[4,8,128]{2,1,0:T(8,128)} %bitcast.97, s32[2,144,128]{2,1,0:T(8,128)} %get-tuple-element.7.packed_ref, f32[8,8,128]{2,1,0:T(8,128)} %get-tuple-element.8.scale_ref), custom_call_target="tpu_custom_call" | custom-call | flops 200000000 | bytes 1000000 | tf_op jit(solution)/shard_map/pairs/pallas_call | solution.py:241
  134.0 0.7 maximum_bitcast_fusion
  134.7 0.6 copy.39
  (40 shorter events, 0.3 us)
Async XLA Ops:
  0.6 12.6 %copy-start.1 = (bf16[384,384]{1,0:T(8,128)(2,1)S(1)}, bf16[384,384]{1,0:T(8,128)(2,1)}, u32[]{:S(2)}) copy-start(bf16[384,384]{1,0:T(8,128)(2,1)} %param.9) | copy-start | bytes 884740
  0.6 7.1 %copy-start.9 = (f32[384]{0:T(512)S(1)}, f32[384]{0:T(512)}, u32[]{:S(2)}) copy-start(f32[384]{0:T(512)} %param.12) | copy-start | bytes 4612
  0.7 7.1 %copy-start.4 = (f32[3,384]{1,0:T(4,128)S(1)}, f32[3,384]{1,0:T(4,128)}, u32[]{:S(2)}) copy-start(f32[3,384]{1,0:T(4,128)} %param.11) | copy-start | bytes 13828
  1.6 37.5 %collective-permute-start.2 = (bf16[192,384]{1,0:T(8,128)(2,1)S(1)}, bf16[192,384]{1,0:T(8,128)(2,1)S(1)}, u32[]{:S(2)}, u32[]{:S(2)}) collective-permute-start(bf16[192,384]{1,0:T(8,128)(2,1)S(1)} %constant_dynamic-slice_fusion.2), channel_id=1, source_target_pairs={{0,24},{8,0},{16,8},{24,16},{1,25},{9,1},{17,9},{25,17},{2,26},{10... | collective-permute-start | bytes 442376 | tf_op jit(solution)/shard_map/ppermute | solution.py:48
  6.8 32.0 %collective-permute-start = (bf16[192,384]{1,0:T(8,128)(2,1)S(1)}, bf16[192,384]{1,0:T(8,128)(2,1)S(1)}, u32[]{:S(2)}, u32[]{:S(2)}) collective-permute-start(bf16[192,384]{1,0:T(8,128)(2,1)S(1)} %constant_dynamic-slice_fusion.2), channel_id=1, source_target_pairs={{0,8},{8,16},{16,24},{24,0},{1,9},{9,17},{17,25},{25,1},{2,10},{10... | collective-permute-start | bytes 442376 | tf_op jit(solution)/shard_map/ppermute | solution.py:48
  6.8 32.6 %collective-permute-start.1 = (bf16[192,384]{1,0:T(8,128)(2,1)S(1)}, bf16[192,384]{1,0:T(8,128)(2,1)S(1)}, u32[]{:S(2)}, u32[]{:S(2)}) collective-permute-start(bf16[192,384]{1,0:T(8,128)(2,1)S(1)} %constant_dynamic-slice_fusion.2), channel_id=1, source_target_pairs={{0,16},{8,24},{16,0},{24,8},{1,17},{9,25},{17,1},{25,9},{2,18},{10... | collective-permute-start | bytes 442376 | tf_op jit(solution)/shard_map/ppermute | solution.py:48
  8.4 4.8 %copy-start.5 = (s32[6,6]{1,0:T(8,128)S(1)}, s32[6,6]{1,0:T(8,128)}, u32[]{:S(2)}) copy-start(s32[6,6]{1,0:T(8,128)} %param.10) | copy-start | bytes 436
  8.4 11.4 %all-to-all-start = ((f32[4,4,384]{2,1,0:T(4,128)}), f32[4,4,384]{2,1,0:T(4,128)S(1)}, u32[]{:S(2)}, u32[]{:S(2)}) async-start(f32[4,4,384]{2,1,0:T(4,128)} %broadcast_in_dim.140), calls=%async_computation | async-start | bytes 49152 | tf_op jit(solution)/shard_map/all_to_all | solution.py:42
  14.0 0.7 copy-start.2
  20.7 3.6 %copy-start.11 = (s32[256,1]{0,1:T(1,128)S(1)}, s32[256,1]{0,1:T(1,128)}, u32[]{:S(2)}) copy-start(s32[256,1]{0,1:T(1,128)} %param.16) | copy-start | bytes 3076
  20.7 13.1 %all-to-all-start.2 = ((bf16[4,384,192]{1,2,0:T(8,128)(2,1)}), bf16[4,384,192]{1,2,0:T(8,128)(2,1)S(1)}, u32[]{:S(2)}, u32[]{:S(2)}) async-start(bf16[4,384,192]{1,2,0:T(8,128)(2,1)} %broadcast_in_dim.148), calls=%async_computation.2 | async-start | bytes 1179648 | tf_op jit(solution)/shard_map/all_to_all | solution.py:42
  24.3 0.7 copy-start.10
  34.6 13.6 %all-to-all-start.1 = ((f32[32,1,1536]{2,1,0:T(1,128)}), f32[32,1,1536]{2,1,0:T(1,128)S(1)}, u32[]{:S(2)}, u32[]{:S(2)}) async-start(f32[32,1,1536]{2,1,0:T(1,128)} %broadcast_in_dim.142), calls=%async_computation.1 | async-start | bytes 393216 | tf_op jit(solution)/shard_map/all_to_all | solution.py:42
  48.1 9.3 %all-to-all-start.3 = ((bf16[2,192,384]{2,1,0:T(8,128)(2,1)}), bf16[2,192,384]{2,1,0:T(8,128)(2,1)S(1)}, u32[]{:S(2)}, u32[]{:S(2)}) async-start(bf16[2,192,384]{2,1,0:T(8,128)(2,1)} %convert_element_type.83), calls=%async_computation.3 | async-start | bytes 589824 | tf_op jit(solution)/shard_map/all_to_all | solution.py:331
  57.6 8.6 %collective-permute-start.3 = (bf16[192,384]{1,0:T(8,128)(2,1)S(1)}, bf16[192,384]{1,0:T(8,128)(2,1)S(1)}, u32[]{:S(2)}, u32[]{:S(2)}) collective-permute-start(bf16[192,384]{1,0:T(8,128)(2,1)S(1)} %fusion.10), channel_id=1, source_target_pairs={{0,8},{8,16},{16,24},{24,0},{1,9},{9,17},{17,25},{25,1},{2,10},{10... | collective-permute-start | bytes 442376 | tf_op jit(solution)/shard_map/ppermute | solution.py:48
  57.7 13.0 %collective-permute-start.4 = (bf16[192,384]{1,0:T(8,128)(2,1)S(1)}, bf16[192,384]{1,0:T(8,128)(2,1)S(1)}, u32[]{:S(2)}, u32[]{:S(2)}) collective-permute-start(bf16[192,384]{1,0:T(8,128)(2,1)S(1)} %fusion.10), channel_id=1, source_target_pairs={{0,16},{8,24},{16,0},{24,8},{1,17},{9,25},{17,1},{25,9},{2,18},{10... | collective-permute-start | bytes 442376 | tf_op jit(solution)/shard_map/ppermute | solution.py:48
  59.5 11.6 %collective-permute-start.5 = (bf16[192,384]{1,0:T(8,128)(2,1)S(1)}, bf16[192,384]{1,0:T(8,128)(2,1)S(1)}, u32[]{:S(2)}, u32[]{:S(2)}) collective-permute-start(bf16[192,384]{1,0:T(8,128)(2,1)S(1)} %fusion.10), channel_id=1, source_target_pairs={{0,24},{8,0},{16,8},{24,16},{1,25},{9,1},{17,9},{25,17},{2,26},{10... | collective-permute-start | bytes 442376 | tf_op jit(solution)/shard_map/ppermute | solution.py:48
  80.4 18.6 %all-to-all-start.5 = ((f32[32,4,8,128]{3,2,1,0:T(8,128)}), f32[32,4,8,128]{3,2,1,0:T(8,128)S(1)}, u32[]{:S(2)}, u32[]{:S(2)}) async-start(f32[32,4,8,128]{3,2,1,0:T(8,128)} %broadcast_in_dim.159), calls=%async_computation.5 | async-start | bytes 1048576 | tf_op jit(solution)/shard_map/all_to_all | solution.py:42
  99.0 0.8 copy-start
  125.9 8.1 %copy-start.6 = (f32[3,2,128]{2,1,0:T(2,128)S(1)}, f32[3,2,128]{2,1,0:T(2,128)}, u32[]{:S(2)}) copy-start(f32[3,2,128]{2,1,0:T(2,128)} %pairs.7) | copy-start | bytes 9220
  125.9 8.1 %copy-start.7 = (f32[3,2,128]{2,1,0:T(2,128)S(1)}, f32[3,2,128]{2,1,0:T(2,128)}, u32[]{:S(2)}) copy-start(f32[3,2,128]{2,1,0:T(2,128)} %pairs.6) | copy-start | bytes 9220
  125.9 8.1 %copy-start.8 = (f32[3,2,128]{2,1,0:T(2,128)S(1)}, f32[3,2,128]{2,1,0:T(2,128)}, u32[]{:S(2)}) copy-start(f32[3,2,128]{2,1,0:T(2,128)} %pairs.5) | copy-start | bytes 9220
  125.9 8.8 %copy-start.3 = (f32[8,1024]{1,0:T(8,128)S(1)}, f32[8,1024]{1,0:T(8,128)}, u32[]{:S(2)}) copy-start(f32[8,1024]{1,0:T(8,128)} %get-tuple-element.9) | copy-start | bytes 98308

commit v2 on v1

--- a/solution.py
+++ b/solution.py
@@ -127,47 +127,61 @@
     )(anchor, own, pick, block, centers)
 
 
-def packing_kernel(ids_ref, near_ref, packed_ref, scale_ref):
-    domains = packed_ref.shape[1] // SUB
-    low = [near_ref[ids_ref[0], c] for c in range(4)]
+SLOT_BITS = 5
+BATCH = 2
+CHUNK = 32
+
+
+def packing_kernel(picks, near_ref, packed_ref, scale_ref):
+    domains = len(picks)
+
+    def entry(d, c):
+        outer, inner = picks[d](near_ref)
+        return near_ref[outer, inner, c]
+
+    low = [entry(0, c) for c in range(4)]
     high = list(low)
     for d in range(1, domains):
         for c in range(4):
-            value = near_ref[ids_ref[d], c]
+            value = entry(d, c)
             low[c] = jnp.minimum(low[c], value)
             high[c] = jnp.maximum(high[c], value)
     steps = 65535.0
-    base, back, step = [], [], []
+    base, back = [], []
     for c in range(4):
         least = jnp.min(low[c], axis=(0, 1), keepdims=True)
         width = jnp.maximum(jnp.max(high[c], axis=(0, 1), keepdims=True) - least, 1e-30)
         base.append(jnp.broadcast_to(least, (SUB, LANES)))
         back.append(jnp.broadcast_to(steps / width, (SUB, LANES)))
-        step.append(jnp.broadcast_to(width * (1.0 / steps), (SUB, LANES)))
         scale_ref[c] = base[c]
-        scale_ref[4 + c] = step[c]
+        scale_ref[4 + c] = jnp.broadcast_to(width * (1.0 / steps), (SUB, LANES))
     for d in range(domains):
         code = [
-            jnp.clip((near_ref[ids_ref[d], c] - base[c]) * back[c] + 0.5, 0.0, steps).astype(
-                jnp.int32
-            )
+            jnp.clip((entry(d, c) - base[c]) * back[c] + 0.5, 0.0, steps).astype(jnp.int32)
             for c in range(4)
         ]
         packed_ref[0, d * SUB : (d + 1) * SUB, :] = code[0] | (code[1] << 16)
         packed_ref[1, d * SUB : (d + 1) * SUB, :] = code[2] | (code[3] << 16)
+    for w in range(2):
+        packed_ref[w, domains * SUB :, :] = jnp.zeros((CHUNK, LANES), jnp.int32)
 
 
 def packing(ids, near):
-    domains = ids.shape[0]
+    domains = ids.shape[1]
+
+    def kernel(ids_ref, near_ref, packed_ref, scale_ref):
+        picks = [lambda _, d=d: (ids_ref[0, d], ids_ref[1, d]) for d in range(domains)]
+        packing_kernel(picks, near_ref, packed_ref, scale_ref)
+
     return pl.pallas_call(
-        packing_kernel,
+        kernel,
         out_shape=(
-            jax.ShapeDtypeStruct((2, domains * SUB, LANES), jnp.int32),
+            jax.ShapeDtypeStruct((2, domains * SUB + CHUNK, LANES), jnp.int32),
             jax.ShapeDtypeStruct((8, SUB, LANES), jnp.float32),
         ),
         in_specs=[pl.BlockSpec(memory_space=SMEM), pl.BlockSpec(memory_space=VMEM)],
         out_specs=(pl.BlockSpec(memory_space=VMEM),) * 2,
-        cost_estimate=pl.CostEstimate(flops=10**7, bytes_accessed=10**6, transcendentals=0),
+        cost_estimate=pl.CostEstimate(flops=10**7, bytes_accessed=5 * 10**6, transcendentals=0),
         name="packing",
     )(ids, near)
 
@@ -180,104 +194,164 @@
     return jnp.zeros_like(place)
 
 
-def pair_kernel(counts, first, groups, lists_ref, own_ref, packed_ref, scale_ref, force_ref):
-    rows = packed_ref.shape[1]
-    parts = lists_ref.shape[1] // SUB
+def places_of(slot):
+    p = (slot * 57) >> 9
+    rest = slot - 9 * p
+    q = (rest * 11) >> 5
+    return p, q, rest - 3 * q
+
+
+def network(count):
+    pairs = []
+    p = 1
+    while p < count:
+        k = p
+        while k >= 1:
+            for j in range(k % p, count - k, 2 * k):
+                for i in range(min(k, count - j - k)):
+                    if (i + j) // (2 * p) == (i + j + k) // (2 * p):
+                        pairs.append((i + j, i + j + k))
+            k //= 2
+        p *= 2
+    return pairs
+
+
+def sorting_kernel(counts, lists_ref, keys_ref, range_ref, spread_ref):
+    entries = lists_ref.shape[1]
     distinct = [min(3, count) for count in counts]
-
-    def group(a, _):
-        column = pl.multiple_of((first + a) * LANES, LANES)
-        mine = [
-            jnp.broadcast_to(own_ref[c, pl.ds(first + a, 1), :], (SUB, LANES)) for c in range(4)
-        ]
-
-        def part(b, sums):
-            start = pl.multiple_of(b * SUB, SUB)
-            slot = lists_ref[0, pl.ds(start, SUB), pl.ds(column, LANES)]
-            member = lists_ref[1, pl.ds(start, SUB), pl.ds(column, LANES)]
-            p = (slot * 57) >> 9
-            rest = slot - 9 * p
-            q = (rest * 11) >> 5
-            r = rest - 3 * q
+    for b in range(entries // SUB):
+        for a in range(SUB):
+            slot = lists_ref[0, b * SUB : (b + 1) * SUB, a * LANES : (a + 1) * LANES]
+            member = lists_ref[1, b * SUB : (b + 1) * SUB, a * LANES : (a + 1) * LANES]
+            p, q, r = places_of(slot)
             domain = (
                 compact(p, counts[0]) * distinct[1] + compact(q, counts[1])
             ) * distinct[2] + compact(r, counts[2])
-            row = domain * SUB + (member >> 7)
-            lane = member & (LANES - 1)
-            words = [jnp.zeros((SUB, LANES), jnp.int32) for _ in range(2)]
-            for k in range(rows):
-                here = row == k
-                for w in range(2):
-                    line = jnp.broadcast_to(packed_ref[w, k : k + 1, :], (SUB, LANES))
-                    words[w] = jnp.where(here, pick_lanes(line, lane), words[w])
+            key = ((domain * (SUB * LANES) + member) << SLOT_BITS) + slot
+            spread_ref[pl.ds(b * SUB * SUB + a, SUB, stride=SUB), :] = key.astype(jnp.float32)
+    keys = [spread_ref[n * SUB : (n + 1) * SUB, :] for n in range(entries)]
+    for i, j in network(entries):
+        keys[i], keys[j] = jnp.minimum(keys[i], keys[j]), jnp.maximum(keys[i], keys[j])
+    for n in range(entries):
+        keys_ref[n] = keys[n].astype(jnp.int32)
+    least = [jnp.min(keys[n], axis=0, keepdims=True) for n in range(0, entries, BATCH)]
+    most = [
+        jnp.max(keys[n + BATCH - 1], axis=0, keepdims=True) for n in range(0, entries, BATCH)
+    ]
+    least = jnp.min(jnp.concatenate(least, axis=0), axis=1, keepdims=True)
+    most = jnp.max(jnp.concatenate(most, axis=0), axis=1, keepdims=True)
+    both = jnp.concatenate([least, most], axis=0).astype(jnp.int32) >> (SLOT_BITS + 7)
+    range_ref[...] = jnp.broadcast_to(both, range_ref.shape)
+
+
+def sorting(counts, lists):
+    entries = lists.shape[1]
+    return pl.pallas_call(
+        functools.partial(sorting_kernel, counts),
+        out_shape=(
+            jax.ShapeDtypeStruct((entries, SUB, LANES), jnp.int32),
+            jax.ShapeDtypeStruct((2 * entries // BATCH, LANES), jnp.int32),
+        ),
+        in_specs=[pl.BlockSpec(memory_space=VMEM)],
+        out_specs=(pl.BlockSpec(memory_space=VMEM),) * 2,
+        scratch_shapes=[pltpu.VMEM((entries * SUB, LANES), jnp.float32)],
+        cost_estimate=pl.CostEstimate(flops=10**7, bytes_accessed=7 * 10**6, transcendentals=0),
+        name="sorting",
+    )(lists)
+
+
+def pair_kernel(first, last, range_ref, keys_ref, own_ref, packed_ref, scale_ref, force_ref):
+    blocks = keys_ref.shape[0] // BATCH
+    mine = [own_ref[c] for c in range(4)]
+
+    def step(j, sums):
+        keys = [keys_ref[j * BATCH + i] for i in range(BATCH)]
+        rows = [key >> (SLOT_BITS + 7) for key in keys]
+        lanes = [(key >> SLOT_BITS) & (LANES - 1) for key in keys]
+        low = range_ref[j, 0]
+        rounds = (range_ref[blocks + j, 0] - low) // CHUNK + 1
+
+        def scan(i, words):
+            words = list(words)
+            base = low + i * CHUNK
+            for m in range(BATCH):
+                for u in range(CHUNK):
+                    here = rows[m] == base + u
+                    for w in range(2):
+                        line = jnp.broadcast_to(packed_ref[w, pl.ds(base + u, 1), :], (SUB, LANES))
+                        k = 2 * m + w
+                        words[k] = jnp.where(here, pick_lanes(line, lanes[m]), words[k])
+            return tuple(words)
+
+        zero = jnp.zeros((SUB, LANES), jnp.int32)
+        words = lax.fori_loop(0, rounds, scan, (zero,) * (2 * BATCH))
+        sums = list(sums)
+        for m in range(BATCH):
+            places = places_of(keys[m] & ((1 << SLOT_BITS) - 1))
             code = [
-                words[0] & 0xFFFF,
-                (words[0] >> 16) & 0xFFFF,
-                words[1] & 0xFFFF,
-                (words[1] >> 16) & 0xFFFF,
+                words[2 * m] & 0xFFFF,
+                (words[2 * m] >> 16) & 0xFFFF,
+                words[2 * m + 1] & 0xFFFF,
+                (words[2 * m + 1] >> 16) & 0xFFFF,
             ]
             value = [code[c].astype(jnp.float32) * scale_ref[4 + c] + scale_ref[c] for c in range(4)]
-            shift = [(place - 1).astype(jnp.float32) * domain_edge for place in (p, q, r)]
+            shift = [(place - 1).astype(jnp.float32) * domain_edge for place in places]
             offset = [mine[c] - (value[c] + shift[c]) for c in range(3)]
             distance = (
                 offset[0] * offset[0] + offset[1] * offset[1] + offset[2] * offset[2] + soften
             )
             inverse = lax.rsqrt(distance)
             strength = value[3] * (inverse * inverse * inverse)
-            return tuple(sums[c] + offset[c] * strength for c in range(3))
-
-        zero = jnp.zeros((SUB, LANES), jnp.float32)
-        sums = lax.fori_loop(0, parts, part, (zero, zero, zero))
-        for c in range(3):
-            force_ref[c, pl.ds(a, 1), :] = (
-                coulomb * mine[3][:1] * jnp.sum(sums[c], axis=0, keepdims=True)
-            )
-        return 0
-
-    lax.fori_loop(0, groups, group, 0)
-
-
-def pair_forces(counts, first, groups, lists, own, packed, scale):
+            for c in range(3):
+                sums[c] = sums[c] + offset[c] * strength
+        return tuple(sums)
+
+    zero = jnp.zeros((SUB, LANES), jnp.float32)
+    sums = lax.fori_loop(first, last, step, (zero, zero, zero))
+    for c in range(3):
+        force_ref[c] = coulomb * mine[3] * sums[c]
+
+
+def pair_forces(first, last, ranges, keys, own, packed, scale):
     return pl.pallas_call(
-        functools.partial(pair_kernel, counts, first, groups),
-        out_shape=jax.ShapeDtypeStruct((3, groups, LANES), jnp.float32),
-        in_specs=[pl.BlockSpec(memory_space=VMEM)] * 4,
+        functools.partial(pair_kernel, first, last),
+        out_shape=jax.ShapeDtypeStruct((3, SUB, LANES), jnp.float32),
+        in_specs=[pl.BlockSpec(memory_space=SMEM)] + [pl.BlockSpec(memory_space=VMEM)] * 4,
         out_specs=pl.BlockSpec(memory_space=VMEM),
         cost_estimate=pl.CostEstimate(
-            flops=10**8 * groups, bytes_accessed=10**6, transcendentals=0
+            flops=10**7, bytes_accessed=(last - first) * 10**6, transcendentals=0
         ),
         name="pairs",
-    )(lists, own, packed, scale)
-
-
-def neighbourhood(block):
-    counts = tuple(lax.axis_size(axis) for axis in ALL)
+    )(ranges, keys, own, packed, scale)
+
+
+def neighbourhood(counts, along_rows):
     here = [lax.axis_index(axis) for axis in ALL]
-    reach = []
-    for count in counts:
-        reach.append((-1, 0, 1) if count >= 3 else (0, 1) if count == 2 else (0,))
-    total = counts[0] * counts[1] * counts[2]
-    if total <= 64:
-        near = everyone(block, ALL)
-        ids = [
-            (((here[0] + i) % counts[0]) * counts[1] + (here[1] + j) % counts[1]) * counts[2]
-            + (here[2] + k) % counts[2]
-            for i in reach[0]
+    reach = [(-1, 0, 1) if n >= 3 else (0, 1) if n == 2 else (0,) for n in counts]
+    if counts[1] * counts[2] <= 16:
+        near = everyone(along_rows, ("qc", "grp"))
+        outer = [
+            ((here[1] + j) % counts[1]) * counts[2] + (here[2] + k) % counts[2]
             for j in reach[1]
             for k in reach[2]
         ]
-        return near, jnp.stack(ids).astype(jnp.int32)
-    near = block[None]
-    for axis, count in reversed(tuple(zip(ALL, counts))):
-        ahead = [((i + 1) % count, i) for i in range(count)]
-        behind = [(i, (i + 1) % count) for i in range(count)]
-        if count >= 3:
-            near = jnp.concatenate(
-                [lax.ppermute(near, axis, behind), near, lax.ppermute(near, axis, ahead)], axis=0
-            )
-        elif count == 2:
-            near = jnp.concatenate([near, lax.ppermute(near, axis, ahead)], axis=0)
-    return near, jnp.arange(near.shape[0], dtype=jnp.int32)
+    else:
+        near = along_rows[None]
+        for axis, count in (("grp", counts[2]), ("qc", counts[1])):
+            ahead = [((i + 1) % count, i) for i in range(count)]
+            behind = [(i, (i + 1) % count) for i in range(count)]
+            if count >= 3:
+                near = jnp.concatenate(
+                    [lax.ppermute(near, axis, behind), near, lax.ppermute(near, axis, ahead)]
+                )
+            elif count == 2:
+                near = jnp.concatenate([near, lax.ppermute(near, axis, ahead)])
+        outer = [jnp.int32(k) for k in range(near.shape[0])]
+    inner = [(here[0] + i) % counts[0] for i in reach[0]]
+    ids = jnp.stack(
+        [jnp.stack([o for _ in inner for o in outer]), jnp.stack([i for i in inner for _ in outer])]
+    )
+    return near, ids.astype(jnp.int32)
 
 
 def per_device(
@@ -294,8 +368,17 @@
     atom_count = atoms.shape[4]
     record_count = emb_atom.shape[0]
 
+    own = atoms.reshape(4, SUB, atom_count // SUB)
+    after = lax.optimization_barrier
+
     basis = jnp.concatenate([basis_centers, occupations[None]], axis=0)
-    basis_all = everyone(basis, "qr")
+    plane = SUB * LANES
+    planes = -(-basis.size // plane)
+    packet = jnp.concatenate(
+        [own, jnp.pad(basis.reshape(-1), (0, planes * plane - basis.size)).reshape(planes, SUB, LANES)]
+    )
+    packets = everyone(packet, "qr")
+    basis_all = packets[:, 4:].reshape(extent, planes * plane)[:, : basis.size]
     centers = (
         jnp.transpose(basis_all.reshape(extent, 4, tile_blocks, BLOCK), (1, 0, 2, 3))
     ).reshape(4, extent * tile_blocks, BLOCK)
@@ -305,8 +388,8 @@
     right_own = lax.dynamic_slice_in_dim(kohn_sham, first, width, 0)
     left = everyone(left_own, "qc")
     rights = rotated(right_own, "qr")
-
-    near, ids = neighbourhood(atoms.reshape(4, SUB, atom_count // SUB))
+    near, ids = neighbourhood(counts, packets[:, :4])
+    keys, ranges = sorting(counts, neighbours[0, 0, 0])
 
     anchor = (
         jnp.stack([grid_row, grid_column, layer]).astype(jnp.float32)[None] * domain_edge
@@ -319,7 +402,6 @@
         centers,
     )
     field_all = everyone(field.reshape(extent * order), ALL)
-    potential = jnp.sum(field_all, axis=0).reshape(extent, order)
 
     keep = jnp.repeat(jnp.repeat(pattern, BLOCK, axis=0), BLOCK, axis=1) == 1
     behind = [(grid_row - k) % extent for k in range(extent)]
@@ -328,18 +410,40 @@
     def swap_layers(part):
         wide = part.reshape(layers, width, order)
         mine = lax.dynamic_index_in_dim(wide, layer, 0, keepdims=False)
+        if layers == 2:
+            theirs = lax.dynamic_index_in_dim(wide, 1 - layer, 0, keepdims=False)
+            got = lax.ppermute(theirs.astype(jnp.bfloat16), "grp", [(0, 1), (1, 0)])[None]
+            return mine, got
         got = lax.all_to_all(
             wide.astype(jnp.bfloat16), "grp", split_axis=0, concat_axis=0, tiled=True
         )
         other = jnp.arange(layers)[:, None, None] != layer
-        return mine + jnp.sum(jnp.where(other, got.astype(jnp.float32), 0.0), axis=0)
+        return mine, jnp.where(other, got, 0)
+
+    def added(mine, got):
+        return mine + jnp.sum(got.astype(jnp.float32), axis=0)
+
+    blocks = keys.shape[0] // BATCH
+    cuts = (0, blocks // 4, 3 * blocks // 4, blocks)
 
     product = jnp.zeros((order, order), jnp.float32)
     for k in range(extent):
         product = product + jnp.dot(lefts[k], rights[k], preferred_element_type=jnp.float32)
     product = jnp.where(keep, product, 0.0)
-    product_rows = swap_layers(product).astype(jnp.bfloat16)
+
+    packed, scale = packing(ids, near)
+
+    mine, got = swap_layers(product)
+    mine, packed = after((mine, packed))
+    pair_one = pair_forces(cuts[0], cuts[1], ranges, keys, own, packed, scale)
+    got, pair_one = after((got, pair_one))
+    product_rows = added(mine, got).astype(jnp.bfloat16)
+    product_rows, packed = after((product_rows, packed))
     products = rotated(product_rows, "qr")
+    pair_two = pair_forces(cuts[1], cuts[2], ranges, keys, own, packed, scale)
+    *received, pair_two = after((*products[1:], pair_two))
+    products = [products[0]] + received
+    potential = jnp.sum(field_all, axis=0).reshape(extent, order)
 
     own_column = lax.dynamic_index_in_dim(potential, grid_column, 0, keepdims=False)
     rows_at = jnp.arange(width)[:, None] + first
@@ -365,7 +469,11 @@
             ).astype(jnp.bfloat16)
         cube = cube + jnp.dot(operand, square, preferred_element_type=jnp.float32)
     cube = jnp.where(keep, cube, 0.0)
-    cube_rows = swap_layers(cube)
+    mine, got = swap_layers(cube)
+    mine, packed = after((mine, packed))
+    pair_three = pair_forces(cuts[2], cuts[3], ranges, keys, own, packed, scale)
+    got, pair_three = after((got, pair_three))
+    cube_rows = added(mine, got)
     row_field = lax.dynamic_slice_in_dim(
         lax.dynamic_index_in_dim(potential, grid_row, 0, keepdims=False), first, width, 0
     )
@@ -375,18 +483,7 @@
     ).astype(jnp.bfloat16)
     sign_step = (0.5 * (3.0 * shifted.astype(jnp.float32) - cube_rows)).astype(jnp.bfloat16)
 
-    own = atoms.reshape(4, SUB, atom_count // SUB)
-    packed, scale = packing(ids, near)
-    lists = neighbours[0, 0, 0]
-    pieces = 4
-    groups = SUB // pieces
-    pair_force = jnp.concatenate(
-        [
-            pair_forces(counts, i * groups, groups, lists, own, packed, scale)
-            for i in range(pieces)
-        ],
-        axis=1,
-    )
+    pair_force = pair_one + pair_two + pair_three
     forces = pair_force.reshape(3, atom_count) + embed_force[:3]
     return (sign_step, forces.reshape(3, 1, 1, 1, atom_count))
 

time: 137 us -> 98.4 us (0.72)
  waiting for transfers between devices: 42.5 us -> 23.4 us
  Pallas kernels: 36.8 us -> 26.5 us
  blocking collectives: 8.03 us -> 0 us
    pallas_call x5, Pallas kernels: 34.1 us -> 23.9 us  [the longest x3 19.6 us: pair_forces(): pl.pallas_call(functools.partial(pair_kernel, first, last), out_shape=jax...]
    all_to_all x4, waiting for transfers between devices: 28.8 us -> 20.7 us  [everyone(): return lax.all_to_all(copies, axes, split_axis=0, concat_axis=0, tiled=True)]
    all_to_all x1 -> x0, blocking collectives: 8.03 us -> none  [swap_layers(): lax.all_to_all(wide.astype(jnp.bfloat16), 'grp', split_axis=0, concat_axi...]
    ppermute x6, waiting for transfers between devices: 8.25 us -> 2.4 us  [rotated(): lax.ppermute(value, axis, [(i, (i + k) % count) for i in range(count)])]
    all_to_all x1 -> x0, waiting for transfers between devices: 5.44 us -> none  [swap_layers(): lax.all_to_all(wide.astype(jnp.bfloat16), 'grp', split_axis=0, concat_axi...]
    all_to_all x1 -> x0, starting transfers between devices: 3.45 us -> none  [swap_layers(): lax.all_to_all(wide.astype(jnp.bfloat16), 'grp', split_axis=0, concat_axi...]
    ppermute x0 -> x2, starting transfers between devices: none -> 2.29 us  [swap_layers(): lax.ppermute(theirs.astype(jnp.bfloat16), 'grp', [(0, 1), (1, 0)])[None]]
    unnamed x26 -> x28, local copies, waits for them, and re-layouts: 3.29 us -> 4.79 us
  transfers between devices with their start and end apart: 11 -> 12, of which waited for: 7 -> 5; matrix products, arithmetic and copies ran while one was open for 9% -> 10% of each run, Pallas kernels for 2% -> 27%
where the time goes in v2:
time: 98.4 us; the launch traced here: 97.5 us
  starting transfers between devices  28.2 us (29%)
  Pallas kernels  26.5 us (27%)
  waiting for transfers between devices  23.4 us (24%)
  local copies, waits for them, and re-layouts  11.8 us (12%)
  other arithmetic  3.48 us (4%)
  matrix products  2.9 us (3%)
  between operations  1.16 us (1%)
    all_to_all x4, waiting for transfers between devices, everyone(): return lax.all_to_all(copies, axes, split_axis=0, concat_axis=0, tiled=True)  20.7 us
    pallas_call x3, Pallas kernels, pair_forces(): pl.pallas_call(functools.partial(pair_kernel, first, last), out_shape=jax...  19.6 us
    all_to_all x4, starting transfers between devices, everyone(): return lax.all_to_all(copies, axes, split_axis=0, concat_axis=0, tiled=True)  17.3 us
    ppermute x6, starting transfers between devices, rotated(): lax.ppermute(value, axis, [(i, (i + k) % count) for i in range(count)])  8.61 us
    unnamed x28, local copies, waits for them, and re-layouts  4.79 us
    broadcast_in_dim x5, local copies, waits for them, and re-layouts, everyone(): copies = jnp.broadcast_to(value[None], (count,) + value.shape)  3.99 us
    pallas_call x1, Pallas kernels, embedding(): pl.pallas_call(records_kernel, out_shape=(jax.ShapeDtypeStruct((blocks, B...  2.66 us
    ppermute x6, waiting for transfers between devices, rotated(): lax.ppermute(value, axis, [(i, (i + k) % count) for i in range(count)])  2.4 us
  transfers between devices with their start and end apart: 12, of which 5 were waited for; matrix products, arithmetic and copies ran while one was open for 10% of the time, Pallas kernels for 27%

profile of v2, /device:TPU:0, one launch (start us, length us, event | category | flops | bytes accessed | tf_op | source)
XLA Modules:
  0.0 97.5 jit_solution(13380156366739032517)
XLA Ops:
  0.7 1.0 %constant_dynamic-slice_fusion.2 = bf16[192,384]{1,0:T(8,128)(2,1)S(1)} fusion(bf16[384,384]{1,0:T(8,128)(2,1)} %param.9, s32[]{:T(128)S(6)} %select_n.142), kind=kLoop, calls=%fused_computation.102 | loop fusion | bytes 294916 | tf_op jit(solution)/shard_map/dynamic_slice | solution.py:388
  1.7 5.1 %collective-permute-start.2 = (bf16[192,384]{1,0:T(8,128)(2,1)S(1)}, bf16[192,384]{1,0:T(8,128)(2,1)S(1)}, u32[]{:S(2)}, u32[]{:S(2)}) collective-permute-start(bf16[192,384]{1,0:T(8,128)(2,1)S(1)} %constant_dynamic-slice_fusion.2), channel_id=1, source_target_pairs={{0,24},{8,0},{16,8},{24,16},{1,25},{9,1},{17,9},{25,17},{2,26},{10... | collective-permute-start | bytes 442376 | tf_op jit(solution)/shard_map/ppermute | solution.py:48
  6.8 1.0 %collective-permute-start = (bf16[192,384]{1,0:T(8,128)(2,1)S(1)}, bf16[192,384]{1,0:T(8,128)(2,1)S(1)}, u32[]{:S(2)}, u32[]{:S(2)}) collective-permute-start(bf16[192,384]{1,0:T(8,128)(2,1)S(1)} %constant_dynamic-slice_fusion.2), channel_id=1, source_target_pairs={{0,8},{8,16},{16,24},{24,0},{1,9},{9,17},{17,25},{25,1},{2,10},{10... | collective-permute-start | bytes 442376 | tf_op jit(solution)/shard_map/ppermute | solution.py:48
  7.8 0.0 copy-start.2
  7.9 0.7 copy-done.2
  8.5 0.6 broadcast_in_dim.129
  9.2 4.1 %all-to-all-start = ((f32[4,6,8,128]{3,2,1,0:T(8,128)}), f32[4,6,8,128]{3,2,1,0:T(8,128)S(1)}, u32[]{:S(2)}, u32[]{:S(2)}) async-start(f32[4,6,8,128]{3,2,1,0:T(8,128)} %broadcast_in_dim.129), calls=%async_computation | async-start | bytes 196608 | tf_op jit(solution)/shard_map/all_to_all | solution.py:42
  13.3 0.1 constant_dynamic-slice_fusion.1
  13.4 0.0 copy-start.8
  13.4 0.7 copy-done.8
  14.1 0.7 copy-done.11
  14.8 0.6 fusion.75.anchor_ref
  15.4 0.1 copy.36
  15.5 5.9 %all-to-all-done = f32[4,6,8,128]{3,2,1,0:T(8,128)S(1)} async-done(((f32[4,6,8,128]{3,2,1,0:T(8,128)}), f32[4,6,8,128]{3,2,1,0:T(8,128)S(1)}, u32[]{:S(2)}, u32[]{:S(2)}) %all-to-all-start) | async-done | bytes 98336 | tf_op jit(solution)/shard_map/all_to_all | solution.py:42
  21.4 0.9 broadcast_in_dim.137
  22.3 3.5 %all-to-all-start.2 = ((bf16[4,384,192]{1,2,0:T(8,128)(2,1)}), bf16[4,384,192]{1,2,0:T(8,128)(2,1)S(1)}, u32[]{:S(2)}, u32[]{:S(2)}) async-start(bf16[4,384,192]{1,2,0:T(8,128)(2,1)} %broadcast_in_dim.137), calls=%async_computation.2 | async-start | bytes 1179648 | tf_op jit(solution)/shard_map/all_to_all | solution.py:42
  26.0 0.6 copy.48
  26.6 0.1 copy.35
  26.7 0.1 broadcast_in_dim.135
  26.8 0.1 eq.109
  26.9 0.2 copy.38
  27.2 0.0 copy-start.10
  27.2 0.7 copy-done.10
  27.8 0.6 add.274
  28.4 0.1 stack.96
  28.5 0.1 stack.91
  28.6 2.3 %sorting.1 = (s32[64,8,128]{2,1,0:T(8,128)}, s32[64,128]{1,0:T(8,128)}) custom-call(s32[2,64,1024]{2,1,0:T(8,128)} %bitcast.97), custom_call_target="tpu_custom_call" | custom-call | flops 10000000 | bytes 7000000 | tf_op jit(solution)/shard_map/sorting/pallas_call | solution.py:249
  30.9 0.6 pad_add_fusion.ids_ref
  31.5 0.1 reshape.173
  31.6 0.6 copy.33.centers_ref
  32.2 2.7 %embedding.1 = (f32[24,64]{1,0:T(8,128)}, f32[8,1024]{1,0:T(8,128)}) custom-call(f32[1,3]{1,0:T(1,128)} %fusion.75.anchor_ref, f32[4,1024]{1,0:T(4,128)} %bitcast.116, s32[1,256]{1,0:T(1,128)} %bitcast.125, s32[1,256]{1,0:T(1,128)} %bitcast.124, f32[4,24,64]{2,1,0:T(8,128)} %copy.33.centers_ref), custom_call_target="tpu_custom_call" | custom-call | flops 1000000000 | bytes 1000000 | tf_op jit(solution)/shard_map/embedding/pallas_call | solution.py:117
  34.9 0.8 broadcast_in_dim.130
  35.7 0.8 broadcast_in_dim.131
  36.5 6.2 %all-to-all-start.1 = ((f32[32,1,1536]{2,1,0:T(1,128)}), f32[32,1,1536]{2,1,0:T(1,128)S(1)}, u32[]{:S(2)}, u32[]{:S(2)}) async-start(f32[32,1,1536]{2,1,0:T(1,128)} %broadcast_in_dim.131), calls=%async_computation.1 | async-start | bytes 393216 | tf_op jit(solution)/shard_map/all_to_all | solution.py:42
  42.7 0.3 fusion.27
  43.0 0.3 convolution_add_fusion.4
  43.3 0.0 slice-start
  43.3 0.3 fusion.21
  43.6 8.7 %all-to-all-done.1 = f32[32,1,1536]{2,1,0:T(1,128)S(1)} async-done(((f32[32,1,1536]{2,1,0:T(1,128)}), f32[32,1,1536]{2,1,0:T(1,128)S(1)}, u32[]{:S(2)}, u32[]{:S(2)}) %all-to-all-start.1) | async-done | bytes 196640 | tf_op jit(solution)/shard_map/all_to_all | solution.py:42
  52.3 0.9 broadcast_in_dim.142
  53.2 3.5 %all-to-all-start.3 = ((f32[8,4,4,8,128]{4,3,2,1,0:T(8,128)}), f32[8,4,4,8,128]{4,3,2,1,0:T(8,128)S(1)}, u32[]{:S(2)}, u32[]{:S(2)}) async-start(f32[8,4,4,8,128]{4,3,2,1,0:T(8,128)} %broadcast_in_dim.142), calls=%async_computation.3 | async-start | bytes 1048576 | tf_op jit(solution)/shard_map/all_to_all | solution.py:42
  56.7 0.3 fusion.2
  57.1 2.0 %collective-permute-start.3 = (bf16[192,384]{1,0:T(8,128)(2,1)S(1)}, bf16[192,384]{1,0:T(8,128)(2,1)S(1)}, u32[]{:S(2)}, u32[]{:S(2)}) collective-permute-start(bf16[192,384]{1,0:T(8,128)(2,1)S(1)} %fusion.17), channel_id=1, source_target_pairs={{0,1},{1,0},{2,3},{3,2},{4,5},{5,4},{6,7},{7,6},{8,9},{9,8},{10,11... | collective-permute-start | bytes 442376 | tf_op jit(solution)/shard_map/ppermute | solution.py:415
  59.1 0.1 reduce_sum.25
  59.2 0.1 fusion.80
  59.4 6.1 %all-to-all-done.3.near_ref = f32[8,4,4,8,128]{4,3,2,1,0:T(8,128)S(1)} async-done(((f32[8,4,4,8,128]{4,3,2,1,0:T(8,128)}), f32[8,4,4,8,128]{4,3,2,1,0:T(8,128)S(1)}, u32[]{:S(2)}, u32[]{:S(2)}) %all-to-all-start.3) | async-done | bytes 524320 | tf_op jit(solution)/shard_map/all_to_all | solution.py:42
  65.5 0.8 copy-done
  66.3 2.0 %packing.1 = (s32[2,176,128]{2,1,0:T(8,128)}, f32[8,8,128]{2,1,0:T(8,128)}) custom-call(s32[2,18]{1,0:T(2,128)} %pad_add_fusion.ids_ref, f32[8,4,4,8,128]{4,3,2,1,0:T(8,128)} %copy-done), custom_call_target="tpu_custom_call" | custom-call | flops 10000000 | bytes 5000000 | tf_op jit(solution)/shard_map/packing/pallas_call | solution.py:176
  68.2 5.3 %pairs.3 = f32[3,8,128]{2,1,0:T(8,128)} custom-call(s32[64,128]{1,0:T(8,128)} %get-tuple-element.25.range_ref, s32[64,8,128]{2,1,0:T(8,128)} %get-tuple-element.26.keys_ref, f32[4,8,128]{2,1,0:T(8,128)} %bitcast.98, s32[2,176,128]{2,1,0:T(8,128)} %get-tuple-element.36.packed_ref, f32[8,8,128]{2,1,0:T(8,128)} %get-tuple-element.28.scale_ref), custom_call_target="tpu_custom_call" | custom-call | flops 10000000 | bytes 8000000 | tf_op jit(solution)/shard_map/pairs/pallas_call | solution.py:316
  73.6 0.1 collective-permute-start.6
  73.7 0.5 collective-permute-start.5
  74.1 1.9 %collective-permute-start.4 = (bf16[192,384]{1,0:T(8,128)(2,1)S(1)}, bf16[192,384]{1,0:T(8,128)(2,1)S(1)}, u32[]{:S(2)}, u32[]{:S(2)}) collective-permute-start(bf16[192,384]{1,0:T(8,128)(2,1)S(1)} %fusion.10), channel_id=1, source_target_pairs={{0,8},{8,16},{16,24},{24,0},{1,9},{9,17},{17,25},{25,1},{2,10},{10... | collective-permute-start | bytes 442376 | tf_op jit(solution)/shard_map/ppermute | solution.py:48
  76.1 9.2 %pairs.4 = f32[3,8,128]{2,1,0:T(8,128)} custom-call(s32[64,128]{1,0:T(8,128)} %get-tuple-element.25.range_ref, s32[64,8,128]{2,1,0:T(8,128)} %get-tuple-element.26.keys_ref, f32[4,8,128]{2,1,0:T(8,128)} %bitcast.99, s32[2,176,128]{2,1,0:T(8,128)} %get-tuple-element.36.packed_ref, f32[8,8,128]{2,1,0:T(8,128)} %get-tuple-element.28.scale_ref), custom_call_target="tpu_custom_call" | custom-call | flops 10000000 | bytes 16000000 | tf_op jit(solution)/shard_map/pairs/pallas_call | solution.py:316
  85.3 0.5 fusion.16
  85.7 2.4 %collective-permute-done.5 = bf16[192,384]{1,0:T(8,128)(2,1)S(1)} collective-permute-done((bf16[192,384]{1,0:T(8,128)(2,1)S(1)}, bf16[192,384]{1,0:T(8,128)(2,1)S(1)}, u32[]{:S(2)}, u32[]{:S(2)}) %collective-permute-start.5) | collective-permute-done | bytes 147488 | tf_op jit(solution)/shard_map/ppermute | solution.py:48
  88.1 0.4 convolution_add_fusion.2
  88.6 0.4 convolution_add_fusion.1
  89.0 0.4 fusion
  89.5 0.3 collective-permute-start.7
  89.8 5.1 %pairs.5 = f32[3,8,128]{2,1,0:T(8,128)} custom-call(s32[64,128]{1,0:T(8,128)} %get-tuple-element.25.range_ref, s32[64,8,128]{2,1,0:T(8,128)} %get-tuple-element.26.keys_ref, f32[4,8,128]{2,1,0:T(8,128)} %bitcast.100, s32[2,176,128]{2,1,0:T(8,128)} %get-tuple-element.36.packed_ref, f32[8,8,128]{2,1,0:T(8,128)} %get-tuple-element.28.scale_ref), custom_call_target="tpu_custom_call" | custom-call | flops 10000000 | bytes 8000000 | tf_op jit(solution)/shard_map/pairs/pallas_call | solution.py:316
  95.0 0.3 collective-permute-done.7
  95.3 0.7 add_bitcast_fusion
  96.0 0.6 copy.39
  96.6 0.8 fusion.9
  (50 shorter events, 0.4 us)
Async XLA Ops:
  0.6 7.2 %copy-start.9 = (f32[384]{0:T(512)S(1)}, f32[384]{0:T(512)}, u32[]{:S(2)}) copy-start(f32[384]{0:T(512)} %param.12) | copy-start | bytes 4612
  0.6 7.2 %copy-start.7 = (f32[3,384]{1,0:T(4,128)S(1)}, f32[3,384]{1,0:T(4,128)}, u32[]{:S(2)}) copy-start(f32[3,384]{1,0:T(4,128)} %param.11) | copy-start | bytes 13828
  0.7 12.6 %copy-start.1 = (bf16[384,384]{1,0:T(8,128)(2,1)S(1)}, bf16[384,384]{1,0:T(8,128)(2,1)}, u32[]{:S(2)}) copy-start(bf16[384,384]{1,0:T(8,128)(2,1)} %param.9) | copy-start | bytes 884740
  1.7 41.7 %collective-permute-start.2 = (bf16[192,384]{1,0:T(8,128)(2,1)S(1)}, bf16[192,384]{1,0:T(8,128)(2,1)S(1)}, u32[]{:S(2)}, u32[]{:S(2)}) collective-permute-start(bf16[192,384]{1,0:T(8,128)(2,1)S(1)} %constant_dynamic-slice_fusion.2), channel_id=1, source_target_pairs={{0,24},{8,0},{16,8},{24,16},{1,25},{9,1},{17,9},{25,17},{2,26},{10... | collective-permute-start | bytes 442376 | tf_op jit(solution)/shard_map/ppermute | solution.py:48
  6.8 49.9 %collective-permute-start.1 = (bf16[192,384]{1,0:T(8,128)(2,1)S(1)}, bf16[192,384]{1,0:T(8,128)(2,1)S(1)}, u32[]{:S(2)}, u32[]{:S(2)}) collective-permute-start(bf16[192,384]{1,0:T(8,128)(2,1)S(1)} %constant_dynamic-slice_fusion.2), channel_id=1, source_target_pairs={{0,16},{8,24},{16,0},{24,8},{1,17},{9,25},{17,1},{25,9},{2,18},{10... | collective-permute-start | bytes 442376 | tf_op jit(solution)/shard_map/ppermute | solution.py:48
  6.8 36.2 %collective-permute-start = (bf16[192,384]{1,0:T(8,128)(2,1)S(1)}, bf16[192,384]{1,0:T(8,128)(2,1)S(1)}, u32[]{:S(2)}, u32[]{:S(2)}) collective-permute-start(bf16[192,384]{1,0:T(8,128)(2,1)S(1)} %constant_dynamic-slice_fusion.2), channel_id=1, source_target_pairs={{0,8},{8,16},{16,24},{24,0},{1,9},{9,17},{17,25},{25,1},{2,10},{10... | collective-permute-start | bytes 442376 | tf_op jit(solution)/shard_map/ppermute | solution.py:48
  7.8 0.7 copy-start.2
  9.2 12.2 %all-to-all-start = ((f32[4,6,8,128]{3,2,1,0:T(8,128)}), f32[4,6,8,128]{3,2,1,0:T(8,128)S(1)}, u32[]{:S(2)}, u32[]{:S(2)}) async-start(f32[4,6,8,128]{3,2,1,0:T(8,128)} %broadcast_in_dim.129), calls=%async_computation | async-start | bytes 196608 | tf_op jit(solution)/shard_map/all_to_all | solution.py:42
  13.4 0.7 copy-start.8
  14.1 0.7 copy-start.11
  21.4 14.2 %copy-start.3 = (f32[4,6,8,128]{3,2,1,0:T(8,128)}, f32[4,6,8,128]{3,2,1,0:T(8,128)S(1)}, u32[]{:S(2)}) copy-start(f32[4,6,8,128]{3,2,1,0:T(8,128)S(1)} %all-to-all-done) | copy-start | bytes 294916
  22.3 13.3 %all-to-all-start.2 = ((bf16[4,384,192]{1,2,0:T(8,128)(2,1)}), bf16[4,384,192]{1,2,0:T(8,128)(2,1)S(1)}, u32[]{:S(2)}, u32[]{:S(2)}) async-start(bf16[4,384,192]{1,2,0:T(8,128)(2,1)} %broadcast_in_dim.137), calls=%async_computation.2 | async-start | bytes 1179648 | tf_op jit(solution)/shard_map/all_to_all | solution.py:42
  27.2 0.7 copy-start.10
  36.5 15.9 %all-to-all-start.1 = ((f32[32,1,1536]{2,1,0:T(1,128)}), f32[32,1,1536]{2,1,0:T(1,128)S(1)}, u32[]{:S(2)}, u32[]{:S(2)}) async-start(f32[32,1,1536]{2,1,0:T(1,128)} %broadcast_in_dim.131), calls=%async_computation.1 | async-start | bytes 393216 | tf_op jit(solution)/shard_map/all_to_all | solution.py:42
  43.3 9.0 %slice-start = ((f32[4,6,8,128]{3,2,1,0:T(8,128)}), f32[4,4,8,128]{3,2,1,0:T(8,128)S(1)}, s32[]{:S(2)}) async-start(f32[4,6,8,128]{3,2,1,0:T(8,128)} %copy-done.3), calls=%async_computation.4 | async-start | bytes 131072 | tf_op jit(solution)/shard_map/slice | solution.py:391
  53.2 12.2 %all-to-all-start.3 = ((f32[8,4,4,8,128]{4,3,2,1,0:T(8,128)}), f32[8,4,4,8,128]{4,3,2,1,0:T(8,128)S(1)}, u32[]{:S(2)}, u32[]{:S(2)}) async-start(f32[8,4,4,8,128]{4,3,2,1,0:T(8,128)} %broadcast_in_dim.142), calls=%async_computation.3 | async-start | bytes 1048576 | tf_op jit(solution)/shard_map/all_to_all | solution.py:42
  57.1 16.5 %collective-permute-start.3 = (bf16[192,384]{1,0:T(8,128)(2,1)S(1)}, bf16[192,384]{1,0:T(8,128)(2,1)S(1)}, u32[]{:S(2)}, u32[]{:S(2)}) collective-permute-start(bf16[192,384]{1,0:T(8,128)(2,1)S(1)} %fusion.17), channel_id=1, source_target_pairs={{0,1},{1,0},{2,3},{3,2},{4,5},{5,4},{6,7},{7,6},{8,9},{9,8},{10,11... | collective-permute-start | bytes 442376 | tf_op jit(solution)/shard_map/ppermute | solution.py:415
  65.5 0.8 copy-start
  73.6 12.1 %collective-permute-start.6 = (bf16[192,384]{1,0:T(8,128)(2,1)S(1)}, bf16[192,384]{1,0:T(8,128)(2,1)S(1)}, u32[]{:S(2)}, u32[]{:S(2)}) collective-permute-start(bf16[192,384]{1,0:T(8,128)(2,1)S(1)} %fusion.10), channel_id=1, source_target_pairs={{0,24},{8,0},{16,8},{24,16},{1,25},{9,1},{17,9},{25,17},{2,26},{10... | collective-permute-start | bytes 442376 | tf_op jit(solution)/shard_map/ppermute | solution.py:48
  73.7 14.4 %collective-permute-start.5 = (bf16[192,384]{1,0:T(8,128)(2,1)S(1)}, bf16[192,384]{1,0:T(8,128)(2,1)S(1)}, u32[]{:S(2)}, u32[]{:S(2)}) collective-permute-start(bf16[192,384]{1,0:T(8,128)(2,1)S(1)} %fusion.10), channel_id=1, source_target_pairs={{0,16},{8,24},{16,0},{24,8},{1,17},{9,25},{17,1},{25,9},{2,18},{10... | collective-permute-start | bytes 442376 | tf_op jit(solution)/shard_map/ppermute | solution.py:48
  74.1 14.0 %collective-permute-start.4 = (bf16[192,384]{1,0:T(8,128)(2,1)S(1)}, bf16[192,384]{1,0:T(8,128)(2,1)S(1)}, u32[]{:S(2)}, u32[]{:S(2)}) collective-permute-start(bf16[192,384]{1,0:T(8,128)(2,1)S(1)} %fusion.10), channel_id=1, source_target_pairs={{0,8},{8,16},{16,24},{24,0},{1,9},{9,17},{17,25},{25,1},{2,10},{10... | collective-permute-start | bytes 442376 | tf_op jit(solution)/shard_map/ppermute | solution.py:48
  89.5 5.8 %collective-permute-start.7 = (bf16[192,384]{1,0:T(8,128)(2,1)S(1)}, bf16[192,384]{1,0:T(8,128)(2,1)S(1)}, u32[]{:S(2)}, u32[]{:S(2)}) collective-permute-start(bf16[192,384]{1,0:T(8,128)(2,1)S(1)} %fusion.18), channel_id=1, source_target_pairs={{0,1},{1,0},{2,3},{3,2},{4,5},{5,4},{6,7},{7,6},{8,9},{9,8},{10,11... | collective-permute-start | bytes 442376 | tf_op jit(solution)/shard_map/ppermute | solution.py:415
  89.8 5.5 %copy-start.4 = (f32[3,8,128]{2,1,0:T(8,128)S(1)}, f32[3,8,128]{2,1,0:T(8,128)}, u32[]{:S(2)}) copy-start(f32[3,8,128]{2,1,0:T(8,128)} %pairs.3) | copy-start | bytes 36868
  89.8 5.5 %copy-start.5 = (f32[3,8,128]{2,1,0:T(8,128)S(1)}, f32[3,8,128]{2,1,0:T(8,128)}, u32[]{:S(2)}) copy-start(f32[3,8,128]{2,1,0:T(8,128)} %pairs.4) | copy-start | bytes 36868
  95.0 1.0 %copy-start.6 = (f32[8,1024]{1,0:T(8,128)S(1)}, f32[8,1024]{1,0:T(8,128)}, u32[]{:S(2)}) copy-start(f32[8,1024]{1,0:T(8,128)} %get-tuple-element.41) | copy-start | bytes 98308

commit v3 on v2

v3 whole, which is shorter than its diff:
```python
import functools

import jax
import jax.numpy as jnp
from jax import lax
from jax.experimental import pallas as pl
from jax.experimental.pallas import tpu as pltpu
from jax.sharding import PartitionSpec as P

BLOCK = 64
SUB, LANES = 8, 128

coulomb = 138.935
hartree_nm = 0.0529177
soften = 0.01
domain_edge = 3.4

ALL = ("qr", "qc", "grp")
VMEM = pltpu.MemorySpace.VMEM
GRANT = 16 << 20
SMEM = pltpu.MemorySpace.SMEM

LANE_PICK = lax.GatherDimensionNumbers(
    offset_dims=(),
    collapsed_slice_dims=(1,),
    start_index_map=(1,),
    operand_batching_dims=(0,),
    start_indices_batching_dims=(0,),
)


def pick_lanes(row, lane):
    return lax.gather(
        row, lane[..., None], LANE_PICK, (1, 1), mode=lax.GatherScatterMode.PROMISE_IN_BOUNDS
    )


def everyone(value, axes):
    count = 1
    for axis in (axes,) if isinstance(axes, str) else axes:
        count *= lax.axis_size(axis)
    copies = jnp.broadcast_to(value[None], (count,) + value.shape)
    return lax.all_to_all(copies, axes, split_axis=0, concat_axis=0, tiled=True)


def rotated(value, axis):
    count = lax.axis_size(axis)
    return [value] + [
        lax.ppermute(value, axis, [(i, (i + k) % count) for i in range(count)])
        for k in range(1, count)
    ]


def thirds(value):
    high = value.astype(jnp.bfloat16)
    rest = value - high.astype(jnp.float32)
    middle = rest.astype(jnp.bfloat16)
    low = (rest - middle.astype(jnp.float32)).astype(jnp.bfloat16)
    return high, middle, low


def prepare_kernel(matrix_ref, atoms_ref, centers_ref, weights_ref, left_ref, right_ref, packet_ref):
    order, width = left_ref.shape
    layer = lax.axis_index("grp")
    right_ref[...] = matrix_ref[pl.ds(pl.multiple_of(layer * width, width), width), :]
    for i in range(order // width):

        @pl.when(layer == i)
        def _():
            left_ref[...] = matrix_ref[:, i * width : (i + 1) * width]

    packet_ref[0:4] = atoms_ref[...]
    lines = order // LANES
    rows = [
        (centers_ref[c : c + 1] if c < 3 else weights_ref[...])[:, n * LANES : (n + 1) * LANES]
        for c in range(4)
        for n in range(lines)
    ]
    planes = packet_ref.shape[0] - 4
    rows = rows + [jnp.zeros((1, LANES), jnp.float32)] * (planes * SUB - len(rows))
    for n in range(planes):
        packet_ref[4 + n] = jnp.concatenate(rows[n * SUB : (n + 1) * SUB], axis=0)


def prepare(width, matrix, atoms, centers, weights):
    order = matrix.shape[0]
    planes = -(-4 * (order // LANES) // SUB)
    return pl.pallas_call(
        prepare_kernel,
        out_shape=(
            jax.ShapeDtypeStruct((order, width), matrix.dtype),
            jax.ShapeDtypeStruct((width, order), matrix.dtype),
            jax.ShapeDtypeStruct((4 + planes, SUB, LANES), jnp.float32),
        ),
        in_specs=[pl.BlockSpec(memory_space=VMEM)] * 4,
        out_specs=(pl.BlockSpec(memory_space=VMEM),) * 3,
        cost_estimate=pl.CostEstimate(flops=10**6, bytes_accessed=10**6, transcendentals=0),
        compiler_params=pltpu.CompilerParams(vmem_limit_bytes=GRANT),
        name="prepare",
    )(matrix, atoms, centers, weights)


def records_kernel(extent, lines, *refs):
    packet_refs = refs[:extent]
    pick_ref, dest_ref, block_ref, field_ref, force_ref = refs[extent:]
    count = pick_ref.shape[1]
    here = [lax.axis_index(axis) for axis in ALL]
    anchor = [place.astype(jnp.float32) * domain_edge for place in here]
    pick, dest, block = pick_ref[...], dest_ref[...], block_ref[...]
    lane, group = pick & (LANES - 1), pick >> 7
    behind = here[0] - dest
    behind = jnp.where(behind < 0, behind + extent, behind)
    iota = functools.partial(lax.broadcasted_iota, jnp.int32)
    one_lane = (iota((LANES, count), 0) == lane).astype(jnp.bfloat16)
    in_group = iota((SUB, count), 0) == group
    half = block >> 1
    odd = (block & 1) == 1
    one_line = (iota((extent * lines, count), 0) == behind * lines + half).astype(jnp.bfloat16)
    one_out = (iota((extent * lines, count), 0) == dest * lines + half).astype(jnp.bfloat16)

    def exact(product, value):
        high, middle, low = thirds(value)
        return product(high) + product(middle) + product(low)

    def dot(contract):
        return lambda other: lambda value: lax.dot_general(
            value, other, (contract, ((), ())), preferred_element_type=jnp.float32
        )

    own = packet_refs[0]
    atoms = jnp.concatenate([own[c] for c in range(4)], axis=0)
    spread = exact(dot(((1,), (0,)))(one_lane), atoms)
    taken = [
        jnp.sum(jnp.where(in_group, spread[c * SUB : (c + 1) * SUB], 0.0), axis=0, keepdims=True)
        for c in range(4)
    ]

    def line(k, n):
        return packet_refs[k][4 + n // SUB, n % SUB : n % SUB + 1, :]

    def chosen(c):
        table = jnp.concatenate(
            [line(k, c * lines + n) for k in range(extent) for n in range(lines)], axis=0
        )
        both = exact(dot(((0,), (0,)))(one_line), table)
        return jnp.where(odd, both[BLOCK:], both[:BLOCK])

    charge = taken[3]
    offset = [taken[c] + anchor[c] - chosen(c) for c in range(3)]
    weight = chosen(3)
    distance = offset[0] * offset[0] + offset[1] * offset[1] + offset[2] * offset[2] + soften
    inverse = lax.rsqrt(distance)
    terms = hartree_nm * charge * inverse
    terms = jnp.concatenate([jnp.where(odd, 0.0, terms), jnp.where(odd, terms, 0.0)], axis=0)
    high, middle, low = thirds(terms)
    field_ref[...] = sum(
        lax.dot_general(one_out, piece, (((1,), (1,)), ((), ())), preferred_element_type=jnp.float32)
        for piece in (high, middle, low)
    )
    strength = weight * (inverse * inverse * inverse)
    pushes = [
        coulomb * charge * jnp.sum(strength * offset[c], axis=0, keepdims=True) for c in range(3)
    ]
    pushes = jnp.concatenate([jnp.where(in_group, push, 0.0) for push in pushes], axis=0)
    total = exact(dot(((1,), (1,)))(one_lane), pushes)
    for c in range(3):
        force_ref[c] = total[c * SUB : (c + 1) * SUB]


def embedding(order, packets, pick, dest, block):
    extent, lines = len(packets), order // LANES
    return pl.pallas_call(
        functools.partial(records_kernel, extent, lines),
        out_shape=(
            jax.ShapeDtypeStruct((extent * lines, LANES), jnp.float32),
            jax.ShapeDtypeStruct((3, SUB, LANES), jnp.float32),
        ),
        in_specs=[pl.BlockSpec(memory_space=VMEM)] * (extent + 3),
        out_specs=(pl.BlockSpec(memory_space=VMEM),) * 2,
        cost_estimate=pl.CostEstimate(flops=10**7, bytes_accessed=5 * 10**6, transcendentals=0),
        compiler_params=pltpu.CompilerParams(vmem_limit_bytes=GRANT),
        name="embedding",
    )(*packets, pick, dest, block)


def field_kernel(parts_ref, rows_ref, columns_ref):
    total = parts_ref[0]
    for k in range(1, parts_ref.shape[0]):
        total = total + parts_ref[k]
    rows_ref[...] = total
    for n in range(total.shape[0]):
        columns_ref[n * LANES : (n + 1) * LANES, :] = jnp.broadcast_to(
            total[n : n + 1], (LANES, LANES)
        ).T


def whole_field(parts):
    lines = parts.shape[1]
    return pl.pallas_call(
        field_kernel,
        out_shape=(
            jax.ShapeDtypeStruct((lines, LANES), jnp.float32),
            jax.ShapeDtypeStruct((lines * LANES, LANES), jnp.float32),
        ),
        in_specs=[pl.BlockSpec(memory_space=VMEM)],
        out_specs=(pl.BlockSpec(memory_space=VMEM),) * 2,
        cost_estimate=pl.CostEstimate(flops=10**6, bytes_accessed=3 * 10**6, transcendentals=0),
        compiler_params=pltpu.CompilerParams(vmem_limit_bytes=GRANT),
        name="field",
    )(parts)


def modulo(value, count):
    return jnp.where(value < 0, value + count, value)


def keep_pattern(pattern_ref, value):
    blocks = pattern_ref.shape[0]
    which = lax.broadcasted_iota(jnp.int32, (1, value.shape[1]), 1) // BLOCK
    out = []
    for a in range(blocks):
        marks = jnp.zeros((1, value.shape[1]), jnp.int32)
        for b in range(blocks):
            marks = jnp.where(which == b, pattern_ref[a, b], marks)
        out.append(jnp.where(marks == 1, value[a * BLOCK : (a + 1) * BLOCK], 0.0))
    return jnp.concatenate(out, axis=0)


def part_outputs(layers, value, hold_ref, mine_ref, send_ref):
    width = mine_ref.shape[0]
    layer = lax.axis_index("grp")
    hold_ref[...] = value
    mine_ref[...] = hold_ref[pl.ds(pl.multiple_of(layer * width, width), width), :]
    if layers == 2:
        send_ref[...] = hold_ref[
            pl.ds(pl.multiple_of((1 - layer) * width, width), width), :
        ].astype(send_ref.dtype)
    else:
        send_ref[...] = value.astype(send_ref.dtype)


def product_kernel(places, pattern_ref, *refs):
    extent = len(refs) - 4 - len(places)
    left_refs, right_refs = refs[: len(places)], refs[len(places) : len(places) + extent]
    mine_ref, send_ref, table_ref, hold_ref = refs[len(places) + extent :]
    row, column = lax.axis_index("qr"), lax.axis_index("qc")
    for left_ref, place in zip(left_refs, places):
        table_ref[place(column)] = left_ref[...]
    total = jnp.zeros(hold_ref.shape, jnp.float32)
    for k in range(extent):
        total = total + jnp.dot(
            table_ref[modulo(row - k, extent)],
            right_refs[k][...],
            preferred_element_type=jnp.float32,
        )
    part_outputs(
        hold_ref.shape[0] // mine_ref.shape[0],
        keep_pattern(pattern_ref, total),
        hold_ref,
        mine_ref,
        send_ref,
    )


def part_shapes(order, width):
    rows = width if order == 2 * width else order
    return (
        jax.ShapeDtypeStruct((width, order), jnp.float32),
        jax.ShapeDtypeStruct((rows, order), jnp.bfloat16),
    )


def product_part(pattern, lefts, places, rights):
    order, width = lefts[0].shape
    inputs = len(lefts) + len(rights)
    return pl.pallas_call(
        functools.partial(product_kernel, places),
        out_shape=part_shapes(order, width)
        + (jax.ShapeDtypeStruct((len(lefts), order, width), jnp.bfloat16),),
        in_specs=[pl.BlockSpec(memory_space=SMEM)] + [pl.BlockSpec(memory_space=VMEM)] * inputs,
        out_specs=(pl.BlockSpec(memory_space=VMEM),) * 3,
        scratch_shapes=[pltpu.VMEM((order, order), jnp.float32)],
        cost_estimate=pl.CostEstimate(
            flops=2 * order * order * width * len(rights),
            bytes_accessed=3 * 10**6,
            transcendentals=0,
        ),
        compiler_params=pltpu.CompilerParams(vmem_limit_bytes=GRANT),
        name="product",
    )(pattern, *lefts, *rights)


def cube_kernel(pattern_ref, table_ref, rows_ref, columns_ref, *refs):
    extent = (len(refs) - 3) // 2
    product_refs, right_refs = refs[:extent], refs[extent : 2 * extent]
    mine_ref, send_ref, hold_ref = refs[2 * extent :]
    width, order = mine_ref.shape
    lines = order // LANES
    row, column, layer = (lax.axis_index(axis) for axis in ALL)
    first = layer * width
    iota = functools.partial(lax.broadcasted_iota, jnp.int32)
    total = jnp.zeros((order, order), jnp.float32)
    for k in range(extent):
        tile = modulo(row - k, extent)
        down = columns_ref[pl.ds(pl.multiple_of(tile * order + first, width), width), :]
        pieces = []
        for n in range(lines):
            spot = slice(n * LANES, (n + 1) * LANES)
            across = rows_ref[pl.ds(column * lines + n, 1), :]
            matrix = right_refs[k][:, spot].astype(jnp.float32)
            on_diagonal = iota((width, LANES), 0) + first == iota((width, LANES), 1) + n * LANES
            corner = jnp.where(on_diagonal & (tile == column), down * down, 0.0)
            piece = product_refs[k][:, spot].astype(jnp.float32) + matrix * (down + across) + corner
            pieces.append(piece.astype(jnp.bfloat16))
        square = jnp.concatenate(pieces, axis=1)
        operand = table_ref[tile]
        if k == 0:
            own = columns_ref[pl.ds(pl.multiple_of(row * order, order), order), :]
            parts = []
            for start in range(0, width, LANES):
                size = min(LANES, width - start)
                shape = (order, size)
                on_diagonal = iota(shape, 0) == iota(shape, 1) + (first + start)
                parts.append(jnp.where(on_diagonal, own[:, :size], 0.0))
            added = parts[0] if len(parts) == 1 else jnp.concatenate(parts, axis=1)
            operand = (operand.astype(jnp.float32) + added).astype(jnp.bfloat16)
        total = total + jnp.dot(operand, square, preferred_element_type=jnp.float32)
    part_outputs(
        order // width, keep_pattern(pattern_ref, total), hold_ref, mine_ref, send_ref
    )


def cube_part(pattern, table, rows, columns, products, rights):
    _, order, width = table.shape
    inputs = 3 + len(products) + len(rights)
    return pl.pallas_call(
        cube_kernel,
        out_shape=part_shapes(order, width),
        in_specs=[pl.BlockSpec(memory_space=SMEM)] + [pl.BlockSpec(memory_space=VMEM)] * inputs,
        out_specs=(pl.BlockSpec(memory_space=VMEM),) * 2,
        scratch_shapes=[pltpu.VMEM((order, order), jnp.float32)],
        cost_estimate=pl.CostEstimate(
            flops=2 * order * order * width * len(rights),
            bytes_accessed=3 * 10**6,
            transcendentals=0,
        ),
        compiler_params=pltpu.CompilerParams(vmem_limit_bytes=GRANT),
        name="cube",
    )(pattern, table, rows, columns, *products, *rights)


def final_kernel(mine_ref, got_ref, right_ref, columns_ref, out_ref):
    width, order = mine_ref.shape
    row, column, layer = (lax.axis_index(axis) for axis in ALL)
    first = layer * width
    down = columns_ref[pl.ds(pl.multiple_of(row * order + first, width), width), :]
    iota = functools.partial(lax.broadcasted_iota, jnp.int32)
    for n in range(order // LANES):
        spot = slice(n * LANES, (n + 1) * LANES)
        on_diagonal = iota((width, LANES), 0) + first == iota((width, LANES), 1) + n * LANES
        added = jnp.where(on_diagonal & (row == column), down, 0.0)
        shifted = (right_ref[:, spot].astype(jnp.float32) + added).astype(jnp.bfloat16)
        cube = mine_ref[:, spot] + got_ref[:, spot].astype(jnp.float32)
        out_ref[:, spot] = (0.5 * (3.0 * shifted.astype(jnp.float32) - cube)).astype(jnp.bfloat16)


def final_step(mine, got, right, columns):
    return pl.pallas_call(
        final_kernel,
        out_shape=jax.ShapeDtypeStruct(mine.shape, jnp.bfloat16),
        in_specs=[pl.BlockSpec(memory_space=VMEM)] * 4,
        out_specs=pl.BlockSpec(memory_space=VMEM),
        cost_estimate=pl.CostEstimate(flops=10**6, bytes_accessed=10**6, transcendentals=0),
        compiler_params=pltpu.CompilerParams(vmem_limit_bytes=GRANT),
        name="final",
    )(mine, got, right, columns)


SLOT_BITS = 5
BATCH = 2
CHUNK = 32


def packing_kernel(pick, domains, near_ref, packed_ref, scale_ref):
    picks = pick()

    def entry(d, c):
        outer, inner = picks[d]
        return near_ref[outer, inner, c]

    low = [entry(0, c) for c in range(4)]
    high = list(low)
    for d in range(1, domains):
        for c in range(4):
            value = entry(d, c)
            low[c] = jnp.minimum(low[c], value)
            high[c] = jnp.maximum(high[c], value)
    steps = 65535.0
    base, back = [], []
    for c in range(4):
        least = jnp.min(low[c], axis=(0, 1), keepdims=True)
        width = jnp.maximum(jnp.max(high[c], axis=(0, 1), keepdims=True) - least, 1e-30)
        base.append(jnp.broadcast_to(least, (SUB, LANES)))
        back.append(jnp.broadcast_to(steps / width, (SUB, LANES)))
        scale_ref[c] = base[c]
        scale_ref[4 + c] = jnp.broadcast_to(width * (1.0 / steps), (SUB, LANES))
    for d in range(domains):
        code = [
            jnp.clip((entry(d, c) - base[c]) * back[c] + 0.5, 0.0, steps).astype(jnp.int32)
            for c in range(4)
        ]
        packed_ref[0, d * SUB : (d + 1) * SUB, :] = code[0] | (code[1] << 16)
        packed_ref[1, d * SUB : (d + 1) * SUB, :] = code[2] | (code[3] << 16)
    for w in range(2):
        packed_ref[w, domains * SUB :, :] = jnp.zeros((CHUNK, LANES), jnp.int32)


def packing(pick, domains, near):
    return pl.pallas_call(
        functools.partial(packing_kernel, pick, domains),
        out_shape=(
            jax.ShapeDtypeStruct((2, domains * SUB + CHUNK, LANES), jnp.int32),
            jax.ShapeDtypeStruct((8, SUB, LANES), jnp.float32),
        ),
        in_specs=[pl.BlockSpec(memory_space=VMEM)],
        out_specs=(pl.BlockSpec(memory_space=VMEM),) * 2,
        cost_estimate=pl.CostEstimate(flops=10**7, bytes_accessed=5 * 10**6, transcendentals=0),
        compiler_params=pltpu.CompilerParams(vmem_limit_bytes=GRANT),
        name="packing",
    )(near)


def compact(place, count):
    if count >= 3:
        return place
    if count == 2:
        return jnp.where(place == 1, 0, 1)
    return jnp.zeros_like(place)


def places_of(slot):
    p = (slot * 57) >> 9
    rest = slot - 9 * p
    q = (rest * 11) >> 5
    return p, q, rest - 3 * q


def network(count):
    pairs = []
    p = 1
    while p < count:
        k = p
        while k >= 1:
            for j in range(k % p, count - k, 2 * k):
                for i in range(min(k, count - j - k)):
                    if (i + j) // (2 * p) == (i + j + k) // (2 * p):
                        pairs.append((i + j, i + j + k))
            k //= 2
        p *= 2
    return pairs


def sorting_kernel(counts, lists_ref, keys_ref, range_ref, spread_ref):
    entries = lists_ref.shape[1]
    distinct = [min(3, count) for count in counts]
    for b in range(entries // SUB):
        for a in range(SUB):
            slot = lists_ref[0, b * SUB : (b + 1) * SUB, a * LANES : (a + 1) * LANES]
            member = lists_ref[1, b * SUB : (b + 1) * SUB, a * LANES : (a + 1) * LANES]
            p, q, r = places_of(slot)
            domain = (
                compact(p, counts[0]) * distinct[1] + compact(q, counts[1])
            ) * distinct[2] + compact(r, counts[2])
            key = ((domain * (SUB * LANES) + member) << SLOT_BITS) + slot
            spread_ref[pl.ds(b * SUB * SUB + a, SUB, stride=SUB), :] = key.astype(jnp.float32)
    keys = [spread_ref[n * SUB : (n + 1) * SUB, :] for n in range(entries)]
    for i, j in network(entries):
        keys[i], keys[j] = jnp.minimum(keys[i], keys[j]), jnp.maximum(keys[i], keys[j])
    for n in range(entries):
        keys_ref[n] = keys[n].astype(jnp.int32)
    least = [jnp.min(keys[n], axis=0, keepdims=True) for n in range(0, entries, BATCH)]
    most = [
        jnp.max(keys[n + BATCH - 1], axis=0, keepdims=True) for n in range(0, entries, BATCH)
    ]
    least = jnp.min(jnp.concatenate(least, axis=0), axis=1, keepdims=True)
    most = jnp.max(jnp.concatenate(most, axis=0), axis=1, keepdims=True)
    both = jnp.concatenate([least, most], axis=0).astype(jnp.int32) >> (SLOT_BITS + 7)
    range_ref[...] = jnp.broadcast_to(both, range_ref.shape)


def sorting(counts, lists):
    entries = lists.shape[1]
    return pl.pallas_call(
        functools.partial(sorting_kernel, counts),
        out_shape=(
            jax.ShapeDtypeStruct((entries, SUB, LANES), jnp.int32),
            jax.ShapeDtypeStruct((2 * entries // BATCH, LANES), jnp.int32),
        ),
        in_specs=[pl.BlockSpec(memory_space=VMEM)],
        out_specs=(pl.BlockSpec(memory_space=VMEM),) * 2,
        scratch_shapes=[pltpu.VMEM((entries * SUB, LANES), jnp.float32)],
        cost_estimate=pl.CostEstimate(flops=10**7, bytes_accessed=7 * 10**6, transcendentals=0),
        compiler_params=pltpu.CompilerParams(vmem_limit_bytes=GRANT),
        name="sorting",
    )(lists)


def pair_kernel(
    first, last, range_ref, keys_ref, own_ref, packed_ref, scale_ref, start_ref, force_ref
):
    blocks = keys_ref.shape[0] // BATCH
    mine = [own_ref[c] for c in range(4)]

    def step(j, sums):
        keys = [keys_ref[j * BATCH + i] for i in range(BATCH)]
        rows = [key >> (SLOT_BITS + 7) for key in keys]
        lanes = [(key >> SLOT_BITS) & (LANES - 1) for key in keys]
        low = range_ref[j, 0]
        rounds = (range_ref[blocks + j, 0] - low) // CHUNK + 1

        def scan(i, words):
            words = list(words)
            base = low + i * CHUNK
            for m in range(BATCH):
                for u in range(CHUNK):
                    here = rows[m] == base + u
                    for w in range(2):
                        line = jnp.broadcast_to(packed_ref[w, pl.ds(base + u, 1), :], (SUB, LANES))
                        k = 2 * m + w
                        words[k] = jnp.where(here, pick_lanes(line, lanes[m]), words[k])
            return tuple(words)

        zero = jnp.zeros((SUB, LANES), jnp.int32)
        words = lax.fori_loop(0, rounds, scan, (zero,) * (2 * BATCH))
        sums = list(sums)
        for m in range(BATCH):
            places = places_of(keys[m] & ((1 << SLOT_BITS) - 1))
            code = [
                words[2 * m] & 0xFFFF,
                (words[2 * m] >> 16) & 0xFFFF,
                words[2 * m + 1] & 0xFFFF,
                (words[2 * m + 1] >> 16) & 0xFFFF,
            ]
            value = [code[c].astype(jnp.float32) * scale_ref[4 + c] + scale_ref[c] for c in range(4)]
            shift = [(place - 1).astype(jnp.float32) * domain_edge for place in places]
            offset = [mine[c] - (value[c] + shift[c]) for c in range(3)]
            distance = (
                offset[0] * offset[0] + offset[1] * offset[1] + offset[2] * offset[2] + soften
            )
            inverse = lax.rsqrt(distance)
            strength = value[3] * (inverse * inverse * inverse)
            for c in range(3):
                sums[c] = sums[c] + offset[c] * strength
        return tuple(sums)

    zero = jnp.zeros((SUB, LANES), jnp.float32)
    sums = lax.fori_loop(first, last, step, (zero, zero, zero))
    for c in range(3):
        force_ref[c] = start_ref[c] + coulomb * mine[3] * sums[c]


def pair_forces(first, last, ranges, keys, own, packed, scale, start):
    return pl.pallas_call(
        functools.partial(pair_kernel, first, last),
        out_shape=jax.ShapeDtypeStruct((3, SUB, LANES), jnp.float32),
        in_specs=[pl.BlockSpec(memory_space=SMEM)] + [pl.BlockSpec(memory_space=VMEM)] * 5,
        out_specs=pl.BlockSpec(memory_space=VMEM),
        cost_estimate=pl.CostEstimate(
            flops=10**7, bytes_accessed=(last - first) * 10**6, transcendentals=0
        ),
        compiler_params=pltpu.CompilerParams(vmem_limit_bytes=GRANT),
        name="pairs",
    )(ranges, keys, own, packed, scale, start)


def neighbourhood(counts, along_rows):
    reach = [(-1, 0, 1) if n >= 3 else (0, 1) if n == 2 else (0,) for n in counts]
    inner = [(-i) % counts[0] for i in reach[0]]
    stacked = jnp.stack(along_rows)
    if counts[1] * counts[2] <= 16:
        near = everyone(stacked, ("qc", "grp"))

        def pick():
            column, layer = lax.axis_index("qc"), lax.axis_index("grp")
            outer = [
                lax.rem(column + (j % counts[1]), counts[1]) * counts[2]
                + lax.rem(layer + k, counts[2])
                for j in reach[1]
                for k in ((k % counts[2]) for k in reach[2])
            ]
            return [(o, i) for i in inner for o in outer]

        return near, pick
    near = stacked[None]
    for axis, count in (("grp", counts[2]), ("qc", counts[1])):
        ahead = [((i + 1) % count, i) for i in range(count)]
        behind = [(i, (i + 1) % count) for i in range(count)]
        if count >= 3:
            near = jnp.concatenate(
                [lax.ppermute(near, axis, behind), near, lax.ppermute(near, axis, ahead)]
            )
        elif count == 2:
            near = jnp.concatenate([near, lax.ppermute(near, axis, ahead)])
    outer = range(near.shape[0])
    return near, lambda: [(o, i) for i in inner for o in outer]


def crossed(value, axis):
    count = lax.axis_size(axis)
    if count & (count - 1):
        return rotated(value, axis), [lambda me, k=k: modulo(me - k, count) for k in range(count)]
    return (
        [value]
        + [lax.ppermute(value, axis, [(i, i ^ k) for i in range(count)]) for k in range(1, count)],
        [lambda me, k=k: me ^ k for k in range(count)],
    )


def per_device(
    kohn_sham, pattern, basis_centers, occupations, atoms, neighbours, emb_atom, emb_dest, emb_block
):
    counts = tuple(lax.axis_size(axis) for axis in ALL)
    layers = counts[2]
    order = kohn_sham.shape[0]
    width = order // layers
    record_count = emb_atom.shape[0]
    own = atoms.reshape(4, SUB, LANES)
    after = lax.optimization_barrier

    left_own, right_own, packet = prepare(width, kohn_sham, own, basis_centers, occupations[None])
    packets = rotated(packet, "qr")
    rights = rotated(right_own, "qr")
    lefts, places = crossed(left_own, "qc")
    keys, ranges = sorting(counts, neighbours[0, 0, 0])
    near, pick = neighbourhood(counts, [piece[:4] for piece in packets])
    domains = min(3, counts[0]) * min(3, counts[1]) * min(3, counts[2])

    field, embed_force = embedding(
        order,
        packets,
        emb_atom.reshape(1, record_count),
        emb_dest.reshape(1, record_count),
        emb_block.reshape(1, record_count),
    )

    def from_layers(send):
        if layers == 2:
            return lax.ppermute(send, "grp", [(0, 1), (1, 0)])
        got = lax.all_to_all(
            send.reshape(layers, width, order), "grp", split_axis=0, concat_axis=0, tiled=True
        )
        other = jnp.arange(layers)[:, None, None] != lax.axis_index("grp")
        return jnp.sum(jnp.where(other, got.astype(jnp.float32), 0.0), axis=0)

    blocks = keys.shape[0] // BATCH
    cuts = (0, blocks // 4, 3 * blocks // 4, blocks)

    mine, send, table = product_part(pattern, lefts, places, rights)
    got = from_layers(send)
    field_all = everyone(field, ALL)

    packed, scale = packing(pick, domains, near)
    mine, packed = after((mine, packed))
    force = pair_forces(cuts[0], cuts[1], ranges, keys, own, packed, scale, embed_force)
    got, force = after((got, force))
    product_rows = (mine + got.astype(jnp.float32)).astype(jnp.bfloat16)
    product_rows, force = after((product_rows, force))
    products = rotated(product_rows, "qr")
    force = pair_forces(cuts[1], cuts[2], ranges, keys, own, packed, scale, force)
    rows, columns = whole_field(field_all)
    *received, force = after((*products[1:], force))
    products = [products[0]] + received

    mine, send = cube_part(pattern, table, rows, columns, products, rights)
    got = from_layers(send)
    mine, force = after((mine, force))
    force = pair_forces(cuts[2], cuts[3], ranges, keys, own, packed, scale, force)
    got, force = after((got, force))
    sign_step = final_step(mine, got, right_own, columns)
    return (sign_step, force.reshape(3, 1, 1, 1, SUB * LANES))


def solution(mesh):
    in_specs = (
        P("qr", "qc"),
        P("qr", "qc"),
        P(None, "qr"),
        P("qr"),
        P(None, "qr", "qc", "grp", None),
        P("qr", "qc", "grp", None, None, None),
        P(("qr", "qc", "grp")),
        P(("qr", "qc", "grp"), None),
        P(("qr", "qc", "grp")),
    )
    out_specs = (P(("qr", "grp"), "qc"), P(None, "qr", "qc", "grp", None))
    return jax.shard_map(
        per_device, mesh=mesh, in_specs=in_specs, out_specs=out_specs, check_vma=False
    )
```

time: 98.4 us -> 77.8 us (0.79)
  waiting for transfers between devices: 23.4 us -> 16.1 us
  local copies, waits for them, and re-layouts: 11.8 us -> 5.78 us
  other arithmetic: 3.48 us -> 0.04 us
  Pallas kernels: 26.5 us -> 23.1 us
  starting transfers between devices: 28.2 us -> 31.3 us
  matrix products: 2.9 us -> 0 us
    all_to_all x4 -> x2, waiting for transfers between devices: 20.7 us -> 0.87 us  [everyone(): return lax.all_to_all(copies, axes, split_axis=0, concat_axis=0, tiled=True)]
    ppermute x6 -> x9, starting transfers between devices: 8.61 us -> 17.7 us  [rotated(): lax.ppermute(value, axis, [(i, (i + k) % count) for i in range(count)])]
    all_to_all x4 -> x2, starting transfers between devices: 17.3 us -> 8.33 us  [everyone(): return lax.all_to_all(copies, axes, split_axis=0, concat_axis=0, tiled=True)]
    ppermute x6 -> x9, waiting for transfers between devices: 2.4 us -> 10 us  [rotated(): lax.ppermute(value, axis, [(i, (i + k) % count) for i in range(count)])]
    ppermute x2 -> x5, waiting for transfers between devices: 0.3 us -> 5.21 us  [the longest x3 5.21 us: crossed(): lax.ppermute(value, axis, [(i, i ^ k) for i in range(count)])]
    ppermute x2 -> x5, starting transfers between devices: 2.29 us -> 5.23 us  [the longest x2 3.09 us: from_layers(): return lax.ppermute(send, 'grp', [(0, 1), (1, 0)])]
    dot_general x8 -> x0, matrix products: 2.9 us -> none  [the longest x4 1.73 us: per_device(): cube = cube + jnp.dot(operand, square, preferred_element_type=jnp.float32)]
    broadcast_in_dim x5 -> x2, local copies, waits for them, and re-layouts: 3.99 us -> 1.57 us  [everyone(): copies = jnp.broadcast_to(value[None], (count,) + value.shape)]
  transfers between devices with their start and end apart: 12 -> 16, of which waited for: 5 -> 7; matrix products, arithmetic and copies ran while one was open for 10% -> 2% of each run, Pallas kernels for 27% -> 27%
where the time goes in v3:
time: 77.8 us; the launch traced here: 77 us
  starting transfers between devices  31.3 us (40%)
  Pallas kernels  23.1 us (30%)
  waiting for transfers between devices  16.1 us (21%)
  local copies, waits for them, and re-layouts  5.78 us (7%)
    pallas_call x3, Pallas kernels, pair_forces(): pl.pallas_call(functools.partial(pair_kernel, first, last), out_shape=jax...  17.9 us
    ppermute x9, starting transfers between devices, rotated(): lax.ppermute(value, axis, [(i, (i + k) % count) for i in range(count)])  17.7 us
    ppermute x9, waiting for transfers between devices, rotated(): lax.ppermute(value, axis, [(i, (i + k) % count) for i in range(count)])  10 us
    all_to_all x2, starting transfers between devices, everyone(): return lax.all_to_all(copies, axes, split_axis=0, concat_axis=0, tiled=True)  8.33 us
    ppermute x3, waiting for transfers between devices, crossed(): lax.ppermute(value, axis, [(i, i ^ k) for i in range(count)])  5.21 us
    unnamed x18, local copies, waits for them, and re-layouts  3.52 us
    ppermute x2, starting transfers between devices, from_layers(): return lax.ppermute(send, 'grp', [(0, 1), (1, 0)])  3.09 us
    ppermute x3, starting transfers between devices, crossed(): lax.ppermute(value, axis, [(i, i ^ k) for i in range(count)])  2.14 us
  transfers between devices with their start and end apart: 16, of which 7 were waited for; matrix products, arithmetic and copies ran while one was open for 2% of the time, Pallas kernels for 27%

profile of v3, /device:TPU:0, one launch (start us, length us, event | category | flops | bytes accessed | tf_op | source)
XLA Modules:
  0.0 77.0 jit_solution(11267228216557208248)
XLA Ops:
  0.6 0.7 broadcast_in_dim.6.weights_ref
  1.3 0.0 copy-start.1
  1.3 1.0 %copy-done.1 = bf16[384,384]{1,0:T(8,128)(2,1)S(1)} copy-done((bf16[384,384]{1,0:T(8,128)(2,1)S(1)}, bf16[384,384]{1,0:T(8,128)(2,1)}, u32[]{:S(2)}) %copy-start.1) | copy-done | bytes 294936
  2.3 0.0 copy-start.2
  2.3 0.7 copy-done.2
  3.0 0.0 copy-start.5
  3.0 0.7 copy-done.5
  3.7 5.1 %collective-permute-start.8 = (f32[6,8,128]{2,1,0:T(8,128)S(1)}, f32[6,8,128]{2,1,0:T(8,128)S(1)}, u32[]{:S(2)}, u32[]{:S(2)}) collective-permute-start(f32[6,8,128]{2,1,0:T(8,128)S(1)} %get-tuple-element.35.refs_0_), channel_id=1, source_target_pairs={{0,24},{8,0},{16,8},{24,16},{1,25},{9,1},{17,9},{25,17},{2,26},{10... | collective-permute-start | bytes 73736 | tf_op jit(solution)/shard_map/ppermute | solution.py:49
  8.9 0.0 collective-permute-start.7
  8.9 1.0 %collective-permute-start.6 = (f32[6,8,128]{2,1,0:T(8,128)S(1)}, f32[6,8,128]{2,1,0:T(8,128)S(1)}, u32[]{:S(2)}, u32[]{:S(2)}) collective-permute-start(f32[6,8,128]{2,1,0:T(8,128)S(1)} %get-tuple-element.35.refs_0_), channel_id=1, source_target_pairs={{0,8},{8,16},{16,24},{24,0},{1,9},{9,17},{17,25},{25,1},{2,10},{10... | collective-permute-start | bytes 73736 | tf_op jit(solution)/shard_map/ppermute | solution.py:49
  9.9 2.8 %collective-permute-start.5 = (bf16[192,384]{1,0:T(8,128)(2,1)S(1)}, bf16[192,384]{1,0:T(8,128)(2,1)S(1)}, u32[]{:S(2)}, u32[]{:S(2)}) collective-permute-start(bf16[192,384]{1,0:T(8,128)(2,1)S(1)} %get-tuple-element.33.refs_4_.right_ref), channel_id=1, source_target_pairs={{0,24},{8,0},{16,8},{24,16},{1,25},{9,1},{17,9},{25,17},{2,26},{10... | collective-permute-start | bytes 442376 | tf_op jit(solution)/shard_map/ppermute | solution.py:49
  12.7 0.0 collective-permute-done.8.refs_3_
  12.7 1.1 %collective-permute-done.7.refs_2_ = f32[6,8,128]{2,1,0:T(8,128)S(1)} collective-permute-done((f32[6,8,128]{2,1,0:T(8,128)S(1)}, f32[6,8,128]{2,1,0:T(8,128)S(1)}, u32[]{:S(2)}, u32[]{:S(2)}) %collective-permute-start.7) | collective-permute-done | bytes 24608 | tf_op jit(solution)/shard_map/ppermute | solution.py:49
  13.8 1.0 %collective-permute-done.6.refs_1_ = f32[6,8,128]{2,1,0:T(8,128)S(1)} collective-permute-done((f32[6,8,128]{2,1,0:T(8,128)S(1)}, f32[6,8,128]{2,1,0:T(8,128)S(1)}, u32[]{:S(2)}, u32[]{:S(2)}) %collective-permute-start.6) | collective-permute-done | bytes 24608 | tf_op jit(solution)/shard_map/ppermute | solution.py:49
  14.8 0.9 %broadcast_in_dim.8 = f32[8,4,4,8,128]{4,3,2,1,0:T(8,128)} broadcast(f32[4,4,8,128]{3,2,1,0:T(8,128)S(1)} %pad_maximum_fusion), dimensions={1,2,3,4} | broadcast | bytes 589824 | tf_op jit(solution)/shard_map/broadcast_in_dim | solution.py:42
  15.6 0.0 copy-start.4
  15.6 4.0 %all-to-all-start.1 = ((f32[8,4,4,8,128]{4,3,2,1,0:T(8,128)}), f32[8,4,4,8,128]{4,3,2,1,0:T(8,128)S(1)}, u32[]{:S(2)}, u32[]{:S(2)}) async-start(f32[8,4,4,8,128]{4,3,2,1,0:T(8,128)} %broadcast_in_dim.8), calls=%async_computation.1 | async-start | bytes 1048576 | tf_op jit(solution)/shard_map/all_to_all | solution.py:43
  19.6 4.0 %collective-permute-start.4 = (bf16[192,384]{1,0:T(8,128)(2,1)S(1)}, bf16[192,384]{1,0:T(8,128)(2,1)S(1)}, u32[]{:S(2)}, u32[]{:S(2)}) collective-permute-start(bf16[192,384]{1,0:T(8,128)(2,1)S(1)} %get-tuple-element.33.refs_4_.right_ref), channel_id=1, source_target_pairs={{0,16},{8,24},{16,0},{24,8},{1,17},{9,25},{17,1},{25,9},{2,18},{10... | collective-permute-start | bytes 442376 | tf_op jit(solution)/shard_map/ppermute | solution.py:49
  23.6 0.0 collective-permute-start.3
  23.6 0.0 copy-start
  23.6 1.5 %collective-permute-start.2 = (bf16[384,192]{1,0:T(8,128)(2,1)S(1)}, bf16[384,192]{1,0:T(8,128)(2,1)S(1)}, u32[]{:S(2)}, u32[]{:S(2)}) collective-permute-start(bf16[384,192]{1,0:T(8,128)(2,1)S(1)} %get-tuple-element.32.refs_0_), channel_id=1, source_target_pairs={{0,6},{2,4},{4,2},{6,0},{1,7},{3,5},{5,3},{7,1},{8,14},{10,12},{12... | collective-permute-start | bytes 442376 | tf_op jit(solution)/shard_map/ppermute | solution.py:614
  25.1 0.6 collective-permute-start.1
  25.7 0.0 collective-permute-done.5.refs_7_
  25.7 0.0 collective-permute-start
  25.7 5.9 %collective-permute-done.4.refs_6_ = bf16[192,384]{1,0:T(8,128)(2,1)S(1)} collective-permute-done((bf16[192,384]{1,0:T(8,128)(2,1)S(1)}, bf16[192,384]{1,0:T(8,128)(2,1)S(1)}, u32[]{:S(2)}, u32[]{:S(2)}) %collective-permute-start.4) | collective-permute-done | bytes 147488 | tf_op jit(solution)/shard_map/ppermute | solution.py:49
  31.6 0.0 collective-permute-done.3.refs_5_
  31.6 0.4 collective-permute-done.2.refs_3_
  32.0 4.8 %collective-permute-done.1.refs_2_ = bf16[384,192]{1,0:T(8,128)(2,1)S(1)} collective-permute-done((bf16[384,192]{1,0:T(8,128)(2,1)S(1)}, bf16[384,192]{1,0:T(8,128)(2,1)S(1)}, u32[]{:S(2)}, u32[]{:S(2)}) %collective-permute-start.1) | collective-permute-done | bytes 147488 | tf_op jit(solution)/shard_map/ppermute | solution.py:614
  36.8 0.0 collective-permute-done.refs_1_
  36.8 0.0 copy-done.4
  36.8 1.3 %product.1 = (f32[192,384]{1,0:T(8,128)S(1)}, bf16[192,384]{1,0:T(8,128)(2,1)S(1)}, bf16[4,384,192]{2,1,0:T(8,128)(2,1)S(1)}) custom-call(s32[6,6]{1,0:T(8,128)S(1)} %copy-done.4, bf16[384,192]{1,0:T(8,128)(2,1)S(1)} %get-tuple-element.32.refs_0_, bf16[384,192]{1,0:T(8,128)(2,1)S(1)} %collective-permute-done.refs_1_, ...), custom_call_target="tpu_custom_call" | custom-call | flops 226492416 | bytes 3000000 | tf_op jit(solution)/shard_map/product/pallas_call | solution.py:276
  38.1 1.5 %collective-permute-start.9 = (bf16[192,384]{1,0:T(8,128)(2,1)S(1)}, bf16[192,384]{1,0:T(8,128)(2,1)S(1)}, u32[]{:S(2)}, u32[]{:S(2)}) collective-permute-start(bf16[192,384]{1,0:T(8,128)(2,1)S(1)} %get-tuple-element.42), channel_id=1, source_target_pairs={{0,1},{1,0},{2,3},{3,2},{4,5},{5,4},{6,7},{7,6},{8,9},{9,8},{10,11... | collective-permute-start | bytes 442376 | tf_op jit(solution)/shard_map/ppermute | solution.py:648
  39.6 0.0 copy-done
  39.6 0.0 copy-start.7
  39.6 0.0 copy-start.8
  39.6 0.6 sorting.1
  40.2 0.0 copy-start.6
  40.2 0.1 copy-done.7
  40.3 0.0 copy-done.8
  40.3 0.6 copy-done.6
  40.9 0.6 embedding.1
  41.5 0.0 all-to-all-done.1.near_ref
  41.5 0.7 broadcast_in_dim.7
  42.2 4.4 %all-to-all-start = ((f32[32,12,128]{2,1,0:T(8,128)}), f32[32,12,128]{2,1,0:T(8,128)S(1)}, u32[]{:S(2)}, u32[]{:S(2)}) async-start(f32[32,12,128]{2,1,0:T(8,128)} %broadcast_in_dim.7), calls=%async_computation | async-start | bytes 524288 | tf_op jit(solution)/shard_map/all_to_all | solution.py:43
  46.6 0.0 copy-start.3
  46.6 0.2 packing.1
  46.9 0.5 copy-done.3
  47.4 4.3 %pairs.3.start_ref = f32[3,8,128]{2,1,0:T(8,128)S(1)} custom-call(s32[64,128]{1,0:T(8,128)S(1)} %get-tuple-element.43.range_ref, s32[64,8,128]{2,1,0:T(8,128)S(1)} %get-tuple-element.44.keys_ref, f32[4,8,128]{2,1,0:T(8,128)S(1)} %bitcast.16, s32[2,176,128]{2,1,0:T(8,128)S(1)} %get-tuple-element.45.packed_ref, f32[8,8,128]{2,1,0:T(8,128)S(1)} %get-tuple-element.46.scale_ref, ...), custom_call_target="tpu_custom_call" | custom-call | flops 10000000 | bytes 8000000 | tf_op jit(solution)/shard_map/pairs/pallas_call | solution.py:563
  51.6 0.0 collective-permute-done.9
  51.7 3.7 %collective-permute-start.12 = (bf16[192,384]{1,0:T(8,128)(2,1)S(1)}, bf16[192,384]{1,0:T(8,128)(2,1)S(1)}, u32[]{:S(2)}, u32[]{:S(2)}) collective-permute-start(bf16[192,384]{1,0:T(8,128)(2,1)S(1)} %add_convert_fusion.refs_0_), channel_id=1, source_target_pairs={{0,24},{8,0},{16,8},{24,16},{1,25},{9,1},{17,9},{25,17},{2,26},{10... | collective-permute-start | bytes 442376 | tf_op jit(solution)/shard_map/ppermute | solution.py:49
  55.4 0.0 collective-permute-start.11
  55.4 1.1 %collective-permute-start.10 = (bf16[192,384]{1,0:T(8,128)(2,1)S(1)}, bf16[192,384]{1,0:T(8,128)(2,1)S(1)}, u32[]{:S(2)}, u32[]{:S(2)}) collective-permute-start(bf16[192,384]{1,0:T(8,128)(2,1)S(1)} %add_convert_fusion.refs_0_), channel_id=1, source_target_pairs={{0,8},{8,16},{16,24},{24,0},{1,9},{9,17},{17,25},{25,1},{2,10},{10... | collective-permute-start | bytes 442376 | tf_op jit(solution)/shard_map/ppermute | solution.py:49
  56.4 0.9 %all-to-all-done.parts_ref = f32[32,12,128]{2,1,0:T(8,128)S(1)} async-done(((f32[32,12,128]{2,1,0:T(8,128)}), f32[32,12,128]{2,1,0:T(8,128)S(1)}, u32[]{:S(2)}, u32[]{:S(2)}) %all-to-all-start) | async-done | bytes 196640 | tf_op jit(solution)/shard_map/all_to_all | solution.py:43
  57.3 0.3 field.1
  57.6 8.9 %pairs.4.start_ref = f32[3,8,128]{2,1,0:T(8,128)S(1)} custom-call(s32[64,128]{1,0:T(8,128)S(1)} %get-tuple-element.43.range_ref, s32[64,8,128]{2,1,0:T(8,128)S(1)} %get-tuple-element.44.keys_ref, f32[4,8,128]{2,1,0:T(8,128)S(1)} %bitcast.17, s32[2,176,128]{2,1,0:T(8,128)S(1)} %get-tuple-element.45.packed_ref, f32[8,8,128]{2,1,0:T(8,128)S(1)} %get-tuple-element.46.scale_ref, ...), custom_call_target="tpu_custom_call" | custom-call | flops 10000000 | bytes 16000000 | tf_op jit(solution)/shard_map/pairs/pallas_call | solution.py:563
  66.5 0.0 collective-permute-done.12.refs_3_
  66.5 2.1 %collective-permute-done.11.refs_2_ = bf16[192,384]{1,0:T(8,128)(2,1)S(1)} collective-permute-done((bf16[192,384]{1,0:T(8,128)(2,1)S(1)}, bf16[192,384]{1,0:T(8,128)(2,1)S(1)}, u32[]{:S(2)}, u32[]{:S(2)}) %collective-permute-start.11) | collective-permute-done | bytes 147488 | tf_op jit(solution)/shard_map/ppermute | solution.py:49
  68.6 0.0 collective-permute-done.10.refs_1_
  68.6 1.4 %cube.1 = (f32[192,384]{1,0:T(8,128)S(1)}, bf16[192,384]{1,0:T(8,128)(2,1)S(1)}) custom-call(s32[6,6]{1,0:T(8,128)S(1)} %copy-done.4, bf16[4,384,192]{2,1,0:T(8,128)(2,1)S(1)} %get-tuple-element.34.table_ref, f32[12,128]{1,0:T(8,128)S(1)} %get-tuple-element.37.rows_ref, f32[1536,128]{1,0:T(8,128)S(1)} %get-tuple-element.38.columns_ref, ...), custom_call_target="tpu_custom_call" | custom-call | flops 226492416 | bytes 3000000 | tf_op jit(solution)/shard_map/cube/pallas_call | solution.py:336
  70.0 1.6 %collective-permute-start.13 = (bf16[192,384]{1,0:T(8,128)(2,1)S(1)}, bf16[192,384]{1,0:T(8,128)(2,1)S(1)}, u32[]{:S(2)}, u32[]{:S(2)}) collective-permute-start(bf16[192,384]{1,0:T(8,128)(2,1)S(1)} %get-tuple-element.58), channel_id=1, source_target_pairs={{0,1},{1,0},{2,3},{3,2},{4,5},{5,4},{6,7},{7,6},{8,9},{9,8},{10,11... | collective-permute-start | bytes 442376 | tf_op jit(solution)/shard_map/ppermute | solution.py:648
  71.6 4.7 %pairs.5 = f32[3,8,128]{2,1,0:T(8,128)} custom-call(s32[64,128]{1,0:T(8,128)S(1)} %get-tuple-element.43.range_ref, s32[64,8,128]{2,1,0:T(8,128)S(1)} %get-tuple-element.44.keys_ref, f32[4,8,128]{2,1,0:T(8,128)S(1)} %bitcast.18, s32[2,176,128]{2,1,0:T(8,128)S(1)} %get-tuple-element.45.packed_ref, f32[8,8,128]{2,1,0:T(8,128)S(1)} %get-tuple-element.46.scale_ref, ...), custom_call_target="tpu_custom_call" | custom-call | flops 10000000 | bytes 8000000 | tf_op jit(solution)/shard_map/pairs/pallas_call | solution.py:563
  76.2 0.0 collective-permute-done.13.got_ref
  76.2 0.8 %final.1 = bf16[192,384]{1,0:T(8,128)(2,1)} custom-call(f32[192,384]{1,0:T(8,128)S(1)} %get-tuple-element.57.mine_ref, bf16[192,384]{1,0:T(8,128)(2,1)S(1)} %collective-permute-done.13.got_ref, bf16[192,384]{1,0:T(8,128)(2,1)S(1)} %get-tuple-element.33.refs_4_.right_ref, f32[1536,128]{1,0:T(8,128)S(1)} %get-tuple-element.38.columns_ref), custom_call_target="tpu_custom_call" | custom-call | flops 1000000 | bytes 1000000 | tf_op jit(solution)/shard_map/final/pallas_call | solution.py:368
  (7 shorter events, 0.1 us)
Async XLA Ops:
  1.3 1.0 %copy-start.1 = (bf16[384,384]{1,0:T(8,128)(2,1)S(1)}, bf16[384,384]{1,0:T(8,128)(2,1)}, u32[]{:S(2)}) copy-start(bf16[384,384]{1,0:T(8,128)(2,1)} %matrix_ref.1) | copy-start | bytes 884740
  2.3 0.7 copy-start.2
  3.0 0.7 copy-start.5
  3.7 9.0 %collective-permute-start.8 = (f32[6,8,128]{2,1,0:T(8,128)S(1)}, f32[6,8,128]{2,1,0:T(8,128)S(1)}, u32[]{:S(2)}, u32[]{:S(2)}) collective-permute-start(f32[6,8,128]{2,1,0:T(8,128)S(1)} %get-tuple-element.35.refs_0_), channel_id=1, source_target_pairs={{0,24},{8,0},{16,8},{24,16},{1,25},{9,1},{17,9},{25,17},{2,26},{10... | collective-permute-start | bytes 73736 | tf_op jit(solution)/shard_map/ppermute | solution.py:49
  8.9 4.9 %collective-permute-start.7 = (f32[6,8,128]{2,1,0:T(8,128)S(1)}, f32[6,8,128]{2,1,0:T(8,128)S(1)}, u32[]{:S(2)}, u32[]{:S(2)}) collective-permute-start(f32[6,8,128]{2,1,0:T(8,128)S(1)} %get-tuple-element.35.refs_0_), channel_id=1, source_target_pairs={{0,16},{8,24},{16,0},{24,8},{1,17},{9,25},{17,1},{25,9},{2,18},{10... | collective-permute-start | bytes 73736 | tf_op jit(solution)/shard_map/ppermute | solution.py:49
  8.9 5.9 %collective-permute-start.6 = (f32[6,8,128]{2,1,0:T(8,128)S(1)}, f32[6,8,128]{2,1,0:T(8,128)S(1)}, u32[]{:S(2)}, u32[]{:S(2)}) collective-permute-start(f32[6,8,128]{2,1,0:T(8,128)S(1)} %get-tuple-element.35.refs_0_), channel_id=1, source_target_pairs={{0,8},{8,16},{16,24},{24,0},{1,9},{9,17},{17,25},{25,1},{2,10},{10... | collective-permute-start | bytes 73736 | tf_op jit(solution)/shard_map/ppermute | solution.py:49
  9.9 15.8 %collective-permute-start.5 = (bf16[192,384]{1,0:T(8,128)(2,1)S(1)}, bf16[192,384]{1,0:T(8,128)(2,1)S(1)}, u32[]{:S(2)}, u32[]{:S(2)}) collective-permute-start(bf16[192,384]{1,0:T(8,128)(2,1)S(1)} %get-tuple-element.33.refs_4_.right_ref), channel_id=1, source_target_pairs={{0,24},{8,0},{16,8},{24,16},{1,25},{9,1},{17,9},{25,17},{2,26},{10... | collective-permute-start | bytes 442376 | tf_op jit(solution)/shard_map/ppermute | solution.py:49
  15.6 21.2 %copy-start.4 = (s32[6,6]{1,0:T(8,128)S(1)}, s32[6,6]{1,0:T(8,128)}, u32[]{:S(2)}) copy-start(s32[6,6]{1,0:T(8,128)} %pattern_ref.3) | copy-start | bytes 436
  15.6 25.9 %all-to-all-start.1 = ((f32[8,4,4,8,128]{4,3,2,1,0:T(8,128)}), f32[8,4,4,8,128]{4,3,2,1,0:T(8,128)S(1)}, u32[]{:S(2)}, u32[]{:S(2)}) async-start(f32[8,4,4,8,128]{4,3,2,1,0:T(8,128)} %broadcast_in_dim.8), calls=%async_computation.1 | async-start | bytes 1048576 | tf_op jit(solution)/shard_map/all_to_all | solution.py:43
  19.6 12.0 %collective-permute-start.4 = (bf16[192,384]{1,0:T(8,128)(2,1)S(1)}, bf16[192,384]{1,0:T(8,128)(2,1)S(1)}, u32[]{:S(2)}, u32[]{:S(2)}) collective-permute-start(bf16[192,384]{1,0:T(8,128)(2,1)S(1)} %get-tuple-element.33.refs_4_.right_ref), channel_id=1, source_target_pairs={{0,16},{8,24},{16,0},{24,8},{1,17},{9,25},{17,1},{25,9},{2,18},{10... | collective-permute-start | bytes 442376 | tf_op jit(solution)/shard_map/ppermute | solution.py:49
  23.6 8.0 %collective-permute-start.3 = (bf16[192,384]{1,0:T(8,128)(2,1)S(1)}, bf16[192,384]{1,0:T(8,128)(2,1)S(1)}, u32[]{:S(2)}, u32[]{:S(2)}) collective-permute-start(bf16[192,384]{1,0:T(8,128)(2,1)S(1)} %get-tuple-element.33.refs_4_.right_ref), channel_id=1, source_target_pairs={{0,8},{8,16},{16,24},{24,0},{1,9},{9,17},{17,25},{25,1},{2,10},{10... | collective-permute-start | bytes 442376 | tf_op jit(solution)/shard_map/ppermute | solution.py:49
  23.6 16.0 %copy-start = (s32[1,1,1,2,64,1024]{5,4,3,2,1,0:T(8,128)S(1)}, s32[1,1,1,2,64,1024]{5,4,3,2,1,0:T(8,128)}, u32[]{:S(2)}) copy-start(s32[1,1,1,2,64,1024]{5,4,3,2,1,0:T(8,128)} %param.14) | copy-start | bytes 1572868
  23.6 8.4 %collective-permute-start.2 = (bf16[384,192]{1,0:T(8,128)(2,1)S(1)}, bf16[384,192]{1,0:T(8,128)(2,1)S(1)}, u32[]{:S(2)}, u32[]{:S(2)}) collective-permute-start(bf16[384,192]{1,0:T(8,128)(2,1)S(1)} %get-tuple-element.32.refs_0_), channel_id=1, source_target_pairs={{0,6},{2,4},{4,2},{6,0},{1,7},{3,5},{5,3},{7,1},{8,14},{10,12},{12... | collective-permute-start | bytes 442376 | tf_op jit(solution)/shard_map/ppermute | solution.py:614
  25.1 11.8 %collective-permute-start.1 = (bf16[384,192]{1,0:T(8,128)(2,1)S(1)}, bf16[384,192]{1,0:T(8,128)(2,1)S(1)}, u32[]{:S(2)}, u32[]{:S(2)}) collective-permute-start(bf16[384,192]{1,0:T(8,128)(2,1)S(1)} %get-tuple-element.32.refs_0_), channel_id=1, source_target_pairs={{0,4},{2,6},{4,0},{6,2},{1,5},{3,7},{5,1},{7,3},{8,12},{10,14},{12... | collective-permute-start | bytes 442376 | tf_op jit(solution)/shard_map/ppermute | solution.py:614
  25.7 11.1 %collective-permute-start = (bf16[384,192]{1,0:T(8,128)(2,1)S(1)}, bf16[384,192]{1,0:T(8,128)(2,1)S(1)}, u32[]{:S(2)}, u32[]{:S(2)}) collective-permute-start(bf16[384,192]{1,0:T(8,128)(2,1)S(1)} %get-tuple-element.32.refs_0_), channel_id=1, source_target_pairs={{0,2},{2,0},{4,6},{6,4},{1,3},{3,1},{5,7},{7,5},{8,10},{10,8},{12,... | collective-permute-start | bytes 442376 | tf_op jit(solution)/shard_map/ppermute | solution.py:614
  38.1 13.5 %collective-permute-start.9 = (bf16[192,384]{1,0:T(8,128)(2,1)S(1)}, bf16[192,384]{1,0:T(8,128)(2,1)S(1)}, u32[]{:S(2)}, u32[]{:S(2)}) collective-permute-start(bf16[192,384]{1,0:T(8,128)(2,1)S(1)} %get-tuple-element.42), channel_id=1, source_target_pairs={{0,1},{1,0},{2,3},{3,2},{4,5},{5,4},{6,7},{7,6},{8,9},{9,8},{10,11... | collective-permute-start | bytes 442376 | tf_op jit(solution)/shard_map/ppermute | solution.py:648
  39.6 0.7 copy-start.7
  39.6 0.7 copy-start.8
  40.2 0.7 copy-start.6
  42.2 15.1 %all-to-all-start = ((f32[32,12,128]{2,1,0:T(8,128)}), f32[32,12,128]{2,1,0:T(8,128)S(1)}, u32[]{:S(2)}, u32[]{:S(2)}) async-start(f32[32,12,128]{2,1,0:T(8,128)} %broadcast_in_dim.7), calls=%async_computation | async-start | bytes 524288 | tf_op jit(solution)/shard_map/all_to_all | solution.py:43
  46.6 0.7 copy-start.3
  51.7 14.8 %collective-permute-start.12 = (bf16[192,384]{1,0:T(8,128)(2,1)S(1)}, bf16[192,384]{1,0:T(8,128)(2,1)S(1)}, u32[]{:S(2)}, u32[]{:S(2)}) collective-permute-start(bf16[192,384]{1,0:T(8,128)(2,1)S(1)} %add_convert_fusion.refs_0_), channel_id=1, source_target_pairs={{0,24},{8,0},{16,8},{24,16},{1,25},{9,1},{17,9},{25,17},{2,26},{10... | collective-permute-start | bytes 442376 | tf_op jit(solution)/shard_map/ppermute | solution.py:49
  55.4 13.3 %collective-permute-start.11 = (bf16[192,384]{1,0:T(8,128)(2,1)S(1)}, bf16[192,384]{1,0:T(8,128)(2,1)S(1)}, u32[]{:S(2)}, u32[]{:S(2)}) collective-permute-start(bf16[192,384]{1,0:T(8,128)(2,1)S(1)} %add_convert_fusion.refs_0_), channel_id=1, source_target_pairs={{0,16},{8,24},{16,0},{24,8},{1,17},{9,25},{17,1},{25,9},{2,18},{10... | collective-permute-start | bytes 442376 | tf_op jit(solution)/shard_map/ppermute | solution.py:49
  55.4 13.3 %collective-permute-start.10 = (bf16[192,384]{1,0:T(8,128)(2,1)S(1)}, bf16[192,384]{1,0:T(8,128)(2,1)S(1)}, u32[]{:S(2)}, u32[]{:S(2)}) collective-permute-start(bf16[192,384]{1,0:T(8,128)(2,1)S(1)} %add_convert_fusion.refs_0_), channel_id=1, source_target_pairs={{0,8},{8,16},{16,24},{24,0},{1,9},{9,17},{17,25},{25,1},{2,10},{10... | collective-permute-start | bytes 442376 | tf_op jit(solution)/shard_map/ppermute | solution.py:49
  70.0 6.2 %collective-permute-start.13 = (bf16[192,384]{1,0:T(8,128)(2,1)S(1)}, bf16[192,384]{1,0:T(8,128)(2,1)S(1)}, u32[]{:S(2)}, u32[]{:S(2)}) collective-permute-start(bf16[192,384]{1,0:T(8,128)(2,1)S(1)} %get-tuple-element.58), channel_id=1, source_target_pairs={{0,1},{1,0},{2,3},{3,2},{4,5},{5,4},{6,7},{7,6},{8,9},{9,8},{10,11... | collective-permute-start | bytes 442376 | tf_op jit(solution)/shard_map/ppermute | solution.py:648
